TPU v7x, 32 devices: a whole 2x2x4 slice. The times are simulated.
32 devices in a mesh: ex: 2 (over core), ey: 16 (over z, y, x).
Axes of the slice: x: 2, y: 2, z: 4, core: 2. Of those that a mesh axis runs over, the one named last changes fastest.
Arguments:
- tokens: bfloat16 [32, 256, 1024], P(('ex', 'ey')), may hold values from -16 to 16
- slot_param: bfloat16 [1024, 32], replicated, may hold values from -0.75 to 0.75
- weight_in: bfloat16 [32, 1024, 4096], P('ey', None, 'ex'), may hold values from -0.1875 to 0.1875
- weight_out: bfloat16 [32, 4096, 1024], P('ey', 'ex'), may hold values from -0.09375 to 0.09375
- grad_out: bfloat16 [32, 256, 1024], P(('ex', 'ey')), may hold values from -6 to 6
Outputs:
- grad_tokens: bfloat16 [32, 256, 1024], P(('ex', 'ey'))
- grad_param: float32 [1024, 32], replicated
- grad_win: bfloat16 [32, 1024, 4096], P('ey', None, 'ex')
- grad_wout: bfloat16 [32, 4096, 1024], P('ey', 'ex')
All inputs are finite; a program needn't handle non-finite values.
Results may differ from a plain program's by a relative error of at most 0.017.
Values may be sent and summed in bfloat16 or wider, within the bound.
No kernel may reach another device: no remote copies, remote signals or barrier semaphores. Data moves between devices by JAX's collectives and lax.ppermute only.
A program may use at most 64 MiB of HBM per device.

v0:
```python
import jax
import jax.numpy as jnp
from jax import lax
from jax.experimental import pallas as pl
from jax.experimental.pallas import tpu as pltpu
from jax.sharding import PartitionSpec as P


def gelu_parts(pre):
    cdf = 0.5 * (1.0 + lax.erf(pre * 0.7071067811865476))
    slope = cdf + pre * jnp.exp(-0.5 * pre * pre) * 0.3989422804014327
    return (pre * cdf, slope)


def softmax_along(values, axis):
    top = jnp.max(values, axis=axis, keepdims=True)
    expo = jnp.exp(values - top)
    return expo / jnp.sum(expo, axis=axis, keepdims=True)


def dot(a, b, contract):
    return lax.dot_general(a, b, (contract, ((), ())), preferred_element_type=jnp.float32)


def in_hbm(value):
    return pltpu.with_memory_space_constraint(value, pltpu.HBM)


NN, NT, TN = ((1,), (0,)), ((1,), (1,)), ((0,), (0,))


def spread(rows, slots, mine, kind):
    row = lax.broadcasted_iota(jnp.int32, (rows, slots), 0)
    slot = lax.broadcasted_iota(jnp.int32, (rows, slots), 1)
    target = (slot // mine) * (2 * mine) + kind * mine + slot % mine
    return jnp.where(row == target, 1.0, 0.0).astype(jnp.bfloat16)


def route_kernel(mine, tok_ref, out_ref, par_ref, sent_ref, disp_ref, comb_ref):
    tok = tok_ref[0]
    slots = par_ref.shape[0]
    logits = dot(par_ref[...], tok, NT)
    dispatch = softmax_along(logits, 1)
    combine = softmax_along(logits, 0)
    disp_ref[0] = dispatch
    comb_ref[0] = combine
    first = dot(spread(2 * slots, slots, mine, 0), dispatch.astype(jnp.bfloat16), NN)
    second = dot(spread(2 * slots, slots, mine, 1), combine.astype(jnp.bfloat16), NN)
    both = dot(first.astype(jnp.bfloat16), tok, NN) + dot(second.astype(jnp.bfloat16), out_ref[0], NN)
    for k in range(slots // mine):
        sent_ref[k, 0] = both[2 * mine * k : 2 * mine * (k + 1)].astype(jnp.bfloat16)


def route_forward(tokens, grad_out, param_t, owners):
    images, patches, width = tokens.shape
    slots = param_t.shape[0]
    mine = slots // owners
    whole = pl.BlockSpec((1, patches, width), lambda i: (i, 0, 0))
    table = pl.BlockSpec((1, slots, patches), lambda i: (i, 0, 0))
    return pl.pallas_call(
        lambda *refs: route_kernel(mine, *refs),
        grid=(images,),
        in_specs=[whole, whole, pl.BlockSpec((slots, width), lambda i: (0, 0))],
        out_specs=[pl.BlockSpec((owners, 1, 2 * mine, width), lambda i: (0, i, 0, 0)), table, table],
        out_shape=[
            jax.ShapeDtypeStruct((owners, images, 2 * mine, width), jnp.bfloat16),
            jax.ShapeDtypeStruct((images, slots, patches), jnp.float32),
            jax.ShapeDtypeStruct((images, slots, patches), jnp.float32),
        ],
        compiler_params=pltpu.CompilerParams(vmem_limit_bytes=16 << 20),
        name="route_forward",
    )(in_hbm(tokens), in_hbm(grad_out), in_hbm(param_t))


def expert_body(experts, chunks, x_ref, win_hbm, wout_hbm, part_ref, hid_ref, dpre_ref, win_v, wout_v, sems):
    step = win_v.shape[2] // chunks
    order = [(e, c) for e in range(experts) for c in range(chunks)]

    def copies(e, c):
        cols = pl.ds(c * step, step)
        return (
            pltpu.make_async_copy(win_hbm.at[e, :, cols], win_v.at[e, :, cols], sems.at[0, e, c]),
            pltpu.make_async_copy(wout_hbm.at[e, cols, :], wout_v.at[e, cols, :], sems.at[1, e, c]),
        )

    def open_chunk(e, c):
        for copy in copies(e, c):
            copy.wait()
        cols = pl.ds(c * step, step)
        return dot(x_ref[e], win_v[e, :, cols], NN), dot(x_ref[experts + e], wout_v[e, cols, :], NT)

    for e, c in order:
        for copy in copies(e, c):
            copy.start()
    ready = open_chunk(*order[0])
    out = grad = None
    for k, (e, c) in enumerate(order):
        pre, back = ready
        if k + 1 < len(order):
            ready = open_chunk(*order[k + 1])
        cols = pl.ds(c * step, step)
        value, slope = gelu_parts(pre)
        hidden = value.astype(jnp.bfloat16)
        dpre = (back * slope).astype(jnp.bfloat16)
        hid_ref[e, :, cols] = hidden
        dpre_ref[e, :, cols] = dpre
        o = dot(hidden, wout_v[e, cols, :], NN)
        d = dot(dpre, win_v[e, :, cols], NT)
        out, grad = (o, d) if c == 0 else (out + o, grad + d)
        if c == chunks - 1:
            part_ref[e] = out
            part_ref[experts + e] = grad


def chunk_count(size, wanted):
    while size % wanted or (size // wanted) % 128 and wanted > 1:
        wanted -= 1
    return wanted


def expert_forward(rows_in, weight_in, weight_out):
    experts, width, hid = weight_in.shape
    rows = rows_in.shape[1]
    chunks = chunk_count(hid, 4)
    vmem = pl.BlockSpec(memory_space=pltpu.VMEM)
    hbm = pl.BlockSpec(memory_space=pl.ANY)
    return pl.pallas_call(
        lambda *refs: expert_body(experts, chunks, *refs),
        in_specs=[vmem, hbm, hbm],
        out_specs=[vmem, vmem, vmem],
        out_shape=[
            jax.ShapeDtypeStruct((2 * experts, rows, width), jnp.float32),
            jax.ShapeDtypeStruct((experts, rows, hid), jnp.bfloat16),
            jax.ShapeDtypeStruct((experts, rows, hid), jnp.bfloat16),
        ],
        scratch_shapes=[
            pltpu.VMEM((experts, width, hid), jnp.bfloat16),
            pltpu.VMEM((experts, hid, width), jnp.bfloat16),
            pltpu.SemaphoreType.DMA((2, experts, chunks)),
        ],
        compiler_params=pltpu.CompilerParams(vmem_limit_bytes=22 << 20),
        name="expert_forward",
    )(rows_in, in_hbm(weight_in), in_hbm(weight_out))


def weight_grad_kernel(x_ref, g_ref, hid_ref, dpre_ref, gin_ref, gout_ref):
    gin_ref[0] = dot(x_ref[0], dpre_ref[0], TN).astype(jnp.bfloat16)
    gout_ref[0] = dot(hid_ref[0], g_ref[0], TN).astype(jnp.bfloat16)


def weight_grads(rows_in, hidden, dpre):
    experts, rows, hid = hidden.shape
    width = rows_in.shape[2]
    chunks = chunk_count(hid, 4)
    step = hid // chunks
    return pl.pallas_call(
        weight_grad_kernel,
        grid=(experts, chunks),
        in_specs=[
            pl.BlockSpec((1, rows, width), lambda e, c: (e, 0, 0)),
            pl.BlockSpec((1, rows, width), lambda e, c: (experts + e, 0, 0)),
            pl.BlockSpec((1, rows, step), lambda e, c: (e, 0, c)),
            pl.BlockSpec((1, rows, step), lambda e, c: (e, 0, c)),
        ],
        out_specs=[
            pl.BlockSpec((1, width, step), lambda e, c: (e, 0, c)),
            pl.BlockSpec((1, step, width), lambda e, c: (e, c, 0)),
        ],
        out_shape=[
            jax.ShapeDtypeStruct((experts, width, hid), jnp.bfloat16),
            jax.ShapeDtypeStruct((experts, hid, width), jnp.bfloat16),
        ],
        compiler_params=pltpu.CompilerParams(vmem_limit_bytes=24 << 20),
        name="weight_grads",
    )(rows_in, rows_in, hidden, dpre)


def swap(value, axis, mask):
    size = lax.axis_size(axis)
    return lax.ppermute(value, axis, [(k, k ^ mask) for k in range(size)])


def is_pow2(n):
    return n & (n - 1) == 0


def sum_bits(acc, axis, first_bit):
    size = lax.axis_size(axis)
    bit = first_bit
    while bit < size:
        sent = acc.astype(jnp.bfloat16)
        own = sent.astype(jnp.float32)
        if 2 * bit < size:
            a, b, c = (swap(sent, axis, m).astype(jnp.float32) for m in (bit, 2 * bit, 3 * bit))
            acc = (own + a) + (b + c)
            bit *= 4
        else:
            acc = own + swap(sent, axis, bit).astype(jnp.float32)
            bit *= 2
    return acc


def sum_everywhere(part):
    ex, ey = lax.axis_size("ex"), lax.axis_size("ey")
    if not (is_pow2(ex) and is_pow2(ey)) or ex < 2 or part.shape[0] % 2:
        return lax.psum(part, ("ex", "ey"))
    half = part.shape[0] // 2
    side = lax.axis_index("ex") % 2
    lo, hi = part[:half], part[half:]
    keep = jnp.where(side == 0, lo, hi).astype(jnp.bfloat16)
    give = jnp.where(side == 0, hi, lo).astype(jnp.bfloat16)
    acc = keep.astype(jnp.float32) + swap(give, "ex", 1).astype(jnp.float32)
    acc = sum_bits(acc, "ex", 2)
    acc = sum_bits(acc, "ey", 1)
    sent = acc.astype(jnp.bfloat16)
    own = sent.astype(jnp.float32)
    other = swap(sent, "ex", 1).astype(jnp.float32)
    return jnp.concatenate((jnp.where(side == 0, own, other), jnp.where(side == 0, other, own)), axis=0)


def gather_ex(value):
    if lax.axis_size("ex") == 2:
        return jnp.stack((value, swap(value, "ex", 1)))
    return lax.all_gather(value, "ex", axis=0)


def scatter_sum_ex(parts):
    if lax.axis_size("ex") == 2:
        got = swap(parts[1].astype(jnp.bfloat16), "ex", 1)
        return (parts[0] + got.astype(jnp.float32)).astype(jnp.bfloat16)
    return lax.psum_scatter(parts.astype(jnp.bfloat16), "ex", scatter_dimension=0)


def per_device(tokens, slot_param, weight_in, weight_out, grad_out):
    ex, ey = lax.axis_size("ex"), lax.axis_size("ey")
    images, _, width = tokens.shape
    slots = slot_param.shape[1]
    mine = slots // ey
    param_t = slot_param.T
    sent, dispatch, combine = route_forward(tokens, grad_out, param_t, ey)
    moved = lax.all_to_all(sent.reshape(ey * images, 2 * mine, width), "ey", split_axis=0, concat_axis=0, tiled=True)
    arrived = gather_ex(moved)
    rows = ex * ey * images
    rows_in = arrived.reshape(rows, 2 * mine, width).transpose(1, 0, 2)
    parts, hidden, dpre = expert_forward(rows_in, weight_in, weight_out)
    summed = scatter_sum_ex(parts.transpose(1, 0, 2).reshape(ex, ey * images, 2 * mine, width))
    back = lax.all_to_all(summed, "ey", split_axis=0, concat_axis=0, tiled=True)
    grad_win, grad_wout = weight_grads(rows_in, hidden, dpre)
    back = back.reshape(ey, images, 2, mine, width).transpose(1, 2, 0, 3, 4).reshape(images, 2, slots, width)
    slot_out = back[:, 0]
    grad_slot = back[:, 1]
    d_combine = jnp.einsum("isd,ipd->isp", slot_out, grad_out, preferred_element_type=jnp.float32)
    d_dispatch = jnp.einsum("isd,ipd->isp", grad_slot, tokens, preferred_element_type=jnp.float32)
    d_logits = dispatch * (d_dispatch - jnp.sum(dispatch * d_dispatch, axis=2, keepdims=True))
    d_logits = d_logits + combine * (
        d_combine - jnp.sum(combine * d_combine, axis=1, keepdims=True)
    )
    logit_grad = d_logits.astype(jnp.bfloat16)
    local_param = jnp.einsum("isp,ipd->sd", logit_grad, tokens, preferred_element_type=jnp.float32)
    grad_param = sum_everywhere(local_param).T
    grad_tokens = jnp.einsum(
        "isp,isd->ipd", dispatch.astype(jnp.bfloat16), grad_slot, preferred_element_type=jnp.float32
    )
    grad_tokens = grad_tokens + jnp.einsum(
        "isp,sd->ipd", logit_grad, param_t, preferred_element_type=jnp.float32
    )
    return (grad_tokens.astype(jnp.bfloat16), grad_param, grad_win, grad_wout)


def solution(mesh):
    in_specs = (
        P(("ex", "ey"), None, None),
        P(),
        P("ey", None, "ex"),
        P("ey", "ex", None),
        P(("ex", "ey"), None, None),
    )
    out_specs = (P(("ex", "ey"), None, None), P(), P("ey", None, "ex"), P("ey", "ex", None))

    return jax.shard_map(per_device, mesh=mesh, in_specs=in_specs, out_specs=out_specs, check_vma=False)
```

profile of v0, /device:TPU:0, one launch (start us, length us, event | category | flops | bytes accessed | tf_op | source)
XLA Modules:
  0.0 67.5 jit_solution(4492056387570006132)
XLA Ops:
  0.6 2.1 %route_forward.1 = (bf16[16,1,4,1024]{3,2,1,0:T(4,128)(2,1)S(1)}, f32[1,32,256]{2,1,0:T(8,128)S(1)}, f32[1,32,256]{2,1,0:T(8,128)S(1)}) custom-call(bf16[1,256,1024]{2,1,0:T(8,128)(2,1)} %refs_0_.1, bf16[1,256,1024]{2,1,0:T(8,128)(2,1)} %refs_1_.2, bf16[32,1024]{1,0:T(8,128)(2,1)} %bitcast.77), custom_call_target="tpu_custom_call" | custom-call | tf_op jit(solution)/shard_map/route_forward/pallas_call | solution.py:60
  2.8 15.9 %all_to_all.10 = bf16[16,4,1024]{2,1,0:T(4,128)(2,1)S(1)} all-to-all(bf16[16,4,1024]{2,1,0:T(4,128)(2,1)S(1)} %bitcast.74), channel_id=1, replica_groups=mesh['ex'=2,'ey'=16] {'ey'}, dimensions={0} | all-to-all | bytes 262144 | tf_op jit(solution)/shard_map/all_to_all | solution.py:241
  18.7 1.3 %collective-permute-done = bf16[16,4,1024]{2,1,0:T(4,128)(2,1)S(1)} collective-permute-done((bf16[16,4,1024]{2,1,0:T(4,128)(2,1)S(1)}, bf16[16,4,1024]{2,1,0:T(4,128)(2,1)S(1)}, u32[]{:S(2)}, u32[]{:S(2)}) %collective-permute-start) | collective-permute-done | bytes 131104 | tf_op jit(solution)/shard_map/ppermute | solution.py:180
  20.4 10.6 %expert_forward.1 = (f32[4,32,1024]{2,1,0:T(8,128)S(1)}, bf16[2,32,2048]{2,1,0:T(8,128)(2,1)S(1)}, bf16[2,32,2048]{2,1,0:T(8,128)(2,1)S(1)}) custom-call(bf16[4,32,1024]{2,1,0:T(8,128)(2,1)S(1)} %bitcast.69, bf16[2,1024,2048]{2,1,0:T(8,128)(2,1)} %refs_1_.3, bf16[2,2048,1024]{2,1,0:T(8,128)(2,1)} %refs_2_.1), custom_call_target="tpu_custom_call" | custom-call | tf_op jit(solution)/shard_map/expert_forward/pallas_call | solution.py:127
  31.0 0.2 collective-permute-start.1
  31.2 1.2 %collective-permute-done.1 = bf16[16,4,1024]{2,0,1:T(8,128)(2,1)S(1)} collective-permute-done((bf16[16,4,1024]{2,0,1:T(8,128)(2,1)S(1)}, bf16[16,4,1024]{2,0,1:T(8,128)(2,1)S(1)}, u32[]{:S(2)}, u32[]{:S(2)}) %collective-permute-start.1) | collective-permute-done | bytes 131104 | tf_op jit(solution)/shard_map/ppermute | solution.py:180
  32.4 0.8 %copy.15 = bf16[16,4,1024]{2,1,0:T(4,128)(2,1)} copy(bf16[16,4,1024]{2,0,1:T(8,128)(2,1)S(1)} %fusion.8) | data formatting | bytes 262144 | tf_op jit(solution)/shard_map/convert_element_type | solution.py:230
  33.2 3.5 %all-to-all-start.1 = ((bf16[16,4,1024]{2,1,0:T(4,128)(2,1)}), bf16[16,4,1024]{2,1,0:T(4,128)(2,1)S(1)}, u32[]{:S(2)}, u32[]{:S(2)}) async-start(bf16[16,4,1024]{2,1,0:T(4,128)(2,1)} %copy.15), calls=%async_computation.1 | async-start | bytes 262144 | tf_op jit(solution)/shard_map/all_to_all | solution.py:247
  36.7 8.0 %all-to-all-done.1 = bf16[16,4,1024]{2,1,0:T(4,128)(2,1)S(1)} async-done(((bf16[16,4,1024]{2,1,0:T(4,128)(2,1)}), bf16[16,4,1024]{2,1,0:T(4,128)(2,1)S(1)}, u32[]{:S(2)}, u32[]{:S(2)}) %all-to-all-start.1) | async-done | bytes 131104 | tf_op jit(solution)/shard_map/all_to_all | solution.py:247
  45.1 0.3 fusion.16
  45.4 0.4 fusion.17
  46.1 1.2 %collective-permute-done.2 = bf16[16,1024]{1,0:T(8,128)(2,1)S(1)} collective-permute-done((bf16[16,1024]{1,0:T(8,128)(2,1)S(1)}, bf16[16,1024]{1,0:T(8,128)(2,1)S(1)}, u32[]{:S(2)}, u32[]{:S(2)}) %collective-permute-start.2) | collective-permute-done | bytes 32800 | tf_op jit(solution)/shard_map/ppermute | solution.py:180
  47.3 0.8 %collective-permute-start.5 = (bf16[16,1024]{1,0:T(8,128)(2,1)S(1)}, bf16[16,1024]{1,0:T(8,128)(2,1)S(1)}, u32[]{:S(2)}, u32[]{:S(2)}) collective-permute-start(bf16[16,1024]{1,0:T(8,128)(2,1)S(1)} %add_convert_fusion.2), channel_id=1, source_target_pairs={{0,3},{1,2},{2,1},{3,0},{4,7},{5,6},{6,5},{7,4},{8,11},{9,10},{10,... | collective-permute-start | bytes 98312 | tf_op jit(solution)/shard_map/ppermute | solution.py:180
  48.1 1.8 %collective-permute-start.4 = (bf16[16,1024]{1,0:T(8,128)(2,1)S(1)}, bf16[16,1024]{1,0:T(8,128)(2,1)S(1)}, u32[]{:S(2)}, u32[]{:S(2)}) collective-permute-start(bf16[16,1024]{1,0:T(8,128)(2,1)S(1)} %add_convert_fusion.2), channel_id=1, source_target_pairs={{0,2},{1,3},{2,0},{3,1},{4,6},{5,7},{6,4},{7,5},{8,10},{9,11},{10,... | collective-permute-start | bytes 98312 | tf_op jit(solution)/shard_map/ppermute | solution.py:180
  50.0 0.9 %collective-permute-start.3 = (bf16[16,1024]{1,0:T(8,128)(2,1)S(1)}, bf16[16,1024]{1,0:T(8,128)(2,1)S(1)}, u32[]{:S(2)}, u32[]{:S(2)}) collective-permute-start(bf16[16,1024]{1,0:T(8,128)(2,1)S(1)} %add_convert_fusion.2), channel_id=1, source_target_pairs={{0,1},{1,0},{2,3},{3,2},{4,5},{5,4},{6,7},{7,6},{8,9},{9,8},{10,11... | collective-permute-start | bytes 98312 | tf_op jit(solution)/shard_map/ppermute | solution.py:180
  50.9 7.8 %weight_grads.1 = (bf16[2,1024,2048]{2,1,0:T(8,128)(2,1)}, bf16[2,2048,1024]{2,1,0:T(8,128)(2,1)}) custom-call(bf16[4,32,1024]{2,1,0:T(8,128)(2,1)S(1)} %bitcast.70, bf16[4,32,1024]{2,1,0:T(8,128)(2,1)S(1)} %bitcast.71, bf16[2,32,2048]{2,1,0:T(8,128)(2,1)S(1)} %get-tuple-element.16.hid_ref, bf16[2,32,2048]{2,1,0:T(8,128)(2,1)S(1)} %get-tuple-element.17.dpre_ref), custom_call_target="tpu_custom_call" | custom-call | tf_op jit(solution)/shard_map/weight_grads/pallas_call | solution.py:156
  58.7 1.6 %collective-permute-start.8 = (bf16[16,1024]{1,0:T(8,128)(2,1)S(1)}, bf16[16,1024]{1,0:T(8,128)(2,1)S(1)}, u32[]{:S(2)}, u32[]{:S(2)}) collective-permute-start(bf16[16,1024]{1,0:T(8,128)(2,1)S(1)} %add_convert_fusion.1), channel_id=1, source_target_pairs={{0,12},{1,13},{2,14},{3,15},{4,8},{5,9},{6,10},{7,11},{8,4},{9,5},... | collective-permute-start | bytes 98312 | tf_op jit(solution)/shard_map/ppermute | solution.py:180
  60.4 0.6 collective-permute-start.7
  61.0 2.2 %collective-permute-start.6 = (bf16[16,1024]{1,0:T(8,128)(2,1)S(1)}, bf16[16,1024]{1,0:T(8,128)(2,1)S(1)}, u32[]{:S(2)}, u32[]{:S(2)}) collective-permute-start(bf16[16,1024]{1,0:T(8,128)(2,1)S(1)} %add_convert_fusion.1), channel_id=1, source_target_pairs={{0,4},{1,5},{2,6},{3,7},{4,0},{5,1},{6,2},{7,3},{8,12},{9,13},{10,... | collective-permute-start | bytes 98312 | tf_op jit(solution)/shard_map/ppermute | solution.py:180
  63.2 0.3 fusion.12
  63.5 1.3 %collective-permute-done.8 = bf16[16,1024]{1,0:T(8,128)(2,1)S(1)} collective-permute-done((bf16[16,1024]{1,0:T(8,128)(2,1)S(1)}, bf16[16,1024]{1,0:T(8,128)(2,1)S(1)}, u32[]{:S(2)}, u32[]{:S(2)}) %collective-permute-start.8) | collective-permute-done | bytes 32800 | tf_op jit(solution)/shard_map/ppermute | solution.py:180
  64.8 0.7 %collective-permute-done.7 = bf16[16,1024]{1,0:T(8,128)(2,1)S(1)} collective-permute-done((bf16[16,1024]{1,0:T(8,128)(2,1)S(1)}, bf16[16,1024]{1,0:T(8,128)(2,1)S(1)}, u32[]{:S(2)}, u32[]{:S(2)}) %collective-permute-start.7) | collective-permute-done | bytes 32800 | tf_op jit(solution)/shard_map/ppermute | solution.py:180
  65.6 1.1 %fusion.1 = bf16[1,256,1024]{2,1,0:T(8,128)(2,1)} fusion(f32[256,1024]{1,0:T(8,128)S(1)} %fusion.12, bf16[32,256]{1,0:T(8,128)(2,1)S(1)} %fusion.20, bf16[1024,32]{0,1:T(8,128)(2,1)S(1)} %copy-done.2), kind=kOutput, calls=%fused_computation.2 | convolution fusion | flops 17301504 | bytes 1654784 | tf_op jit(solution)/shard_map/isp,sd->ipd/dot_general | solution.py:264
  66.8 0.7 maximum_bitcast_fusion
  (28 shorter events, 1.3 us)
Async XLA Ops:
  18.7 1.3 %collective-permute-start = (bf16[16,4,1024]{2,1,0:T(4,128)(2,1)S(1)}, bf16[16,4,1024]{2,1,0:T(4,128)(2,1)S(1)}, u32[]{:S(2)}, u32[]{:S(2)}) collective-permute-start(bf16[16,4,1024]{2,1,0:T(4,128)(2,1)S(1)} %all_to_all.10), channel_id=1, source_target_pairs={{0,16},{16,0},{1,17},{17,1},{2,18},{18,2},{3,19},{19,3},{4,20},{20... | collective-permute-start | bytes 393224 | tf_op jit(solution)/shard_map/ppermute | solution.py:180
  20.3 24.7 %copy-start.1 = (bf16[1,256,1024]{2,1,0:T(8,128)(2,1)S(1)}, bf16[1,256,1024]{2,1,0:T(8,128)(2,1)}, u32[]{:S(2)}) copy-start(bf16[1,256,1024]{2,1,0:T(8,128)(2,1)} %refs_1_.2) | copy-start | bytes 1572868
  20.3 25.0 %copy-start = (bf16[1,256,1024]{2,1,0:T(8,128)(2,1)S(1)}, bf16[1,256,1024]{2,1,0:T(8,128)(2,1)}, u32[]{:S(2)}) copy-start(bf16[1,256,1024]{2,1,0:T(8,128)(2,1)} %refs_0_.1) | copy-start | bytes 1572868
  20.4 45.2 %copy-start.2 = (bf16[1024,32]{0,1:T(8,128)(2,1)S(1)}, bf16[1024,32]{0,1:T(8,128)(2,1)}, u32[]{:S(2)}) copy-start(bf16[1024,32]{0,1:T(8,128)(2,1)} %param.6) | copy-start | bytes 196612
  31.0 1.4 %collective-permute-start.1 = (bf16[16,4,1024]{2,0,1:T(8,128)(2,1)S(1)}, bf16[16,4,1024]{2,0,1:T(8,128)(2,1)S(1)}, u32[]{:S(2)}, u32[]{:S(2)}) collective-permute-start(bf16[16,4,1024]{2,0,1:T(8,128)(2,1)S(1)} %slice.45), channel_id=1, source_target_pairs={{0,16},{16,0},{1,17},{17,1},{2,18},{18,2},{3,19},{19,3},{4,20},{20... | collective-permute-start | bytes 393224 | tf_op jit(solution)/shard_map/ppermute | solution.py:180
  33.2 11.5 %all-to-all-start.1 = ((bf16[16,4,1024]{2,1,0:T(4,128)(2,1)}), bf16[16,4,1024]{2,1,0:T(4,128)(2,1)S(1)}, u32[]{:S(2)}, u32[]{:S(2)}) async-start(bf16[16,4,1024]{2,1,0:T(4,128)(2,1)} %copy.15), calls=%async_computation.1 | async-start | bytes 262144 | tf_op jit(solution)/shard_map/all_to_all | solution.py:247
  46.0 1.3 %collective-permute-start.2 = (bf16[16,1024]{1,0:T(8,128)(2,1)S(1)}, bf16[16,1024]{1,0:T(8,128)(2,1)S(1)}, u32[]{:S(2)}, u32[]{:S(2)}) collective-permute-start(bf16[16,1024]{1,0:T(8,128)(2,1)S(1)} %select_convert_fusion), channel_id=1, source_target_pairs={{0,16},{16,0},{1,17},{17,1},{2,18},{18,2},{3,19},{19,3},{4,20},{20... | collective-permute-start | bytes 98312 | tf_op jit(solution)/shard_map/ppermute | solution.py:180
  47.3 11.4 %collective-permute-start.5 = (bf16[16,1024]{1,0:T(8,128)(2,1)S(1)}, bf16[16,1024]{1,0:T(8,128)(2,1)S(1)}, u32[]{:S(2)}, u32[]{:S(2)}) collective-permute-start(bf16[16,1024]{1,0:T(8,128)(2,1)S(1)} %add_convert_fusion.2), channel_id=1, source_target_pairs={{0,3},{1,2},{2,1},{3,0},{4,7},{5,6},{6,5},{7,4},{8,11},{9,10},{10,... | collective-permute-start | bytes 98312 | tf_op jit(solution)/shard_map/ppermute | solution.py:180
  48.1 10.6 %collective-permute-start.4 = (bf16[16,1024]{1,0:T(8,128)(2,1)S(1)}, bf16[16,1024]{1,0:T(8,128)(2,1)S(1)}, u32[]{:S(2)}, u32[]{:S(2)}) collective-permute-start(bf16[16,1024]{1,0:T(8,128)(2,1)S(1)} %add_convert_fusion.2), channel_id=1, source_target_pairs={{0,2},{1,3},{2,0},{3,1},{4,6},{5,7},{6,4},{7,5},{8,10},{9,11},{10,... | collective-permute-start | bytes 98312 | tf_op jit(solution)/shard_map/ppermute | solution.py:180
  50.0 8.8 %collective-permute-start.3 = (bf16[16,1024]{1,0:T(8,128)(2,1)S(1)}, bf16[16,1024]{1,0:T(8,128)(2,1)S(1)}, u32[]{:S(2)}, u32[]{:S(2)}) collective-permute-start(bf16[16,1024]{1,0:T(8,128)(2,1)S(1)} %add_convert_fusion.2), channel_id=1, source_target_pairs={{0,1},{1,0},{2,3},{3,2},{4,5},{5,4},{6,7},{7,6},{8,9},{9,8},{10,11... | collective-permute-start | bytes 98312 | tf_op jit(solution)/shard_map/ppermute | solution.py:180
  58.7 6.0 %collective-permute-start.8 = (bf16[16,1024]{1,0:T(8,128)(2,1)S(1)}, bf16[16,1024]{1,0:T(8,128)(2,1)S(1)}, u32[]{:S(2)}, u32[]{:S(2)}) collective-permute-start(bf16[16,1024]{1,0:T(8,128)(2,1)S(1)} %add_convert_fusion.1), channel_id=1, source_target_pairs={{0,12},{1,13},{2,14},{3,15},{4,8},{5,9},{6,10},{7,11},{8,4},{9,5},... | collective-permute-start | bytes 98312 | tf_op jit(solution)/shard_map/ppermute | solution.py:180
  60.4 5.1 %collective-permute-start.7 = (bf16[16,1024]{1,0:T(8,128)(2,1)S(1)}, bf16[16,1024]{1,0:T(8,128)(2,1)S(1)}, u32[]{:S(2)}, u32[]{:S(2)}) collective-permute-start(bf16[16,1024]{1,0:T(8,128)(2,1)S(1)} %add_convert_fusion.1), channel_id=1, source_target_pairs={{0,8},{1,9},{2,10},{3,11},{4,12},{5,13},{6,14},{7,15},{8,0},{9,1},... | collective-permute-start | bytes 98312 | tf_op jit(solution)/shard_map/ppermute | solution.py:180
  61.0 4.5 %collective-permute-start.6 = (bf16[16,1024]{1,0:T(8,128)(2,1)S(1)}, bf16[16,1024]{1,0:T(8,128)(2,1)S(1)}, u32[]{:S(2)}, u32[]{:S(2)}) collective-permute-start(bf16[16,1024]{1,0:T(8,128)(2,1)S(1)} %add_convert_fusion.1), channel_id=1, source_target_pairs={{0,4},{1,5},{2,6},{3,7},{4,0},{5,1},{6,2},{7,3},{8,12},{9,13},{10,... | collective-permute-start | bytes 98312 | tf_op jit(solution)/shard_map/ppermute | solution.py:180
  65.5 1.3 %collective-permute-start.9 = (bf16[16,1024]{1,0:T(8,128)(2,1)S(1)}, bf16[16,1024]{1,0:T(8,128)(2,1)S(1)}, u32[]{:S(2)}, u32[]{:S(2)}) collective-permute-start(bf16[16,1024]{1,0:T(8,128)(2,1)S(1)} %add_convert_fusion), channel_id=1, source_target_pairs={{0,16},{16,0},{1,17},{17,1},{2,18},{18,2},{3,19},{19,3},{4,20},{20... | collective-permute-start | bytes 98312 | tf_op jit(solution)/shard_map/ppermute | solution.py:180
where the time goes:
time: 67.7 us; the launch traced here: 67.5 us
  Pallas kernels  20.5 us (30%)
  blocking collectives  15.9 us (23%)
  waiting for transfers between devices  13.8 us (20%)
  starting transfers between devices  11.9 us (18%)
  matrix products  2.28 us (3%)
  local copies, waits for them, and re-layouts  1.22 us (2%)
  other arithmetic  1.04 us (2%)
  between operations  0.82 us (1%)
    all_to_all x1, blocking collectives, per_device(): lax.all_to_all(sent.reshape(ey * images, 2 * mine, width), 'ey', split_ax...  15.9 us
    pallas_call x1, Pallas kernels, expert_forward(): pl.pallas_call(lambda *refs: expert_body(experts, chunks, *refs), in_spec...  10.6 us
    ppermute x10, starting transfers between devices, swap(): return lax.ppermute(value, axis, [(k, k ^ mask) for k in range(size)])  8.36 us
    all_to_all x1, waiting for transfers between devices, per_device(): back = lax.all_to_all(summed, 'ey', split_axis=0, concat_axis=0, tiled=True)  7.98 us
    pallas_call x1, Pallas kernels, weight_grads(): pl.pallas_call(weight_grad_kernel, grid=(experts, chunks), in_specs=[pl.B...  7.81 us
    ppermute x10, waiting for transfers between devices, swap(): return lax.ppermute(value, axis, [(k, k ^ mask) for k in range(size)])  5.8 us
    all_to_all x1, starting transfers between devices, per_device(): back = lax.all_to_all(summed, 'ey', split_axis=0, concat_axis=0, tiled=True)  3.51 us
    pallas_call x1, Pallas kernels, route_forward(): pl.pallas_call(lambda *refs: route_kernel(mine, *refs), grid=(images,), i...  2.13 us
  transfers between devices with their start and end apart: 11, of which 7 were waited for; matrix products, arithmetic and copies ran while one was open for 2% of the time, Pallas kernels for 12%

commit v1 on v0

v1 whole, which is shorter than its diff:
```python
import jax
import jax.numpy as jnp
from jax import lax
from jax.experimental import pallas as pl
from jax.experimental.pallas import tpu as pltpu
from jax.sharding import PartitionSpec as P


def gelu_parts(pre):
    cdf = 0.5 * (1.0 + lax.erf(pre * 0.7071067811865476))
    slope = cdf + pre * jnp.exp(-0.5 * pre * pre) * 0.3989422804014327
    return (pre * cdf, slope)


def softmax_along(values, axis):
    top = jnp.max(values, axis=axis, keepdims=True)
    expo = jnp.exp(values - top)
    return expo / jnp.sum(expo, axis=axis, keepdims=True)


def dot(a, b, contract):
    return lax.dot_general(a, b, (contract, ((), ())), preferred_element_type=jnp.float32)


def in_hbm(value):
    return pltpu.with_memory_space_constraint(value, pltpu.HBM)


NN, NT, TN = ((1,), (0,)), ((1,), (1,)), ((0,), (0,))


def chunk_count(size, wanted):
    while size % wanted or (size // wanted) % 256 and wanted > 1:
        wanted -= 1
    return wanted


CHUNKS, AHEAD, FLIGHT = 8, 3, 4


def first_columns(hid):
    chunks = chunk_count(hid, CHUNKS)
    return min(AHEAD, chunks) * (hid // chunks)


def row_kind(shape, mine):
    return (lax.broadcasted_iota(jnp.int32, shape, 0) // mine) % 2


def slot_rows(slots, mine, wide, kind=None):
    shape = (2 * slots, slots) if wide else (slots, 2 * slots)
    row = lax.broadcasted_iota(jnp.int32, shape, 0 if wide else 1)
    slot = lax.broadcasted_iota(jnp.int32, shape, 1 if wide else 0)
    hit = (row // (2 * mine)) * mine + row % mine == slot
    if kind is not None:
        hit = hit & ((row // mine) % 2 == kind)
    return jnp.where(hit, 1.0, 0.0).astype(jnp.bfloat16)


def route_kernel(
    mine, tok_hbm, out_hbm, par_hbm, win_hbm, wout_hbm,
    sent_ref, mix_ref, win_v, wout_v, tok_v, out_v, par_v, sems,
):
    slots, first = par_v.shape[0], win_v.shape[1]
    loads = [
        pltpu.make_async_copy(par_hbm, par_v, sems.at[0]),
        pltpu.make_async_copy(tok_hbm, tok_v, sems.at[1]),
        pltpu.make_async_copy(out_hbm, out_v, sems.at[2]),
        pltpu.make_async_copy(win_hbm.at[0, :, pl.ds(0, first)], win_v, sems.at[3]),
        pltpu.make_async_copy(wout_hbm.at[0, pl.ds(0, first), :], wout_v, sems.at[4]),
    ]
    for load in loads:
        load.start()
    loads[0].wait()
    par = dot(slot_rows(slots, mine, True), par_v[...], NN).astype(jnp.bfloat16)
    loads[1].wait()
    for image in range(tok_v.shape[0]):
        tok = tok_v[image]
        logits = dot(par, tok, NT)
        dispatch = softmax_along(logits, 1)
        expo = jnp.exp(logits - jnp.max(logits, axis=0, keepdims=True))
        combine = expo / (0.5 * jnp.sum(expo, axis=0, keepdims=True))
        is_in = row_kind(logits.shape, mine) == 0
        mix_ref[image] = jnp.where(is_in, dispatch, combine)
        left = jnp.where(is_in, dispatch, 0.0).astype(jnp.bfloat16)
        right = jnp.where(is_in, 0.0, combine).astype(jnp.bfloat16)
        both = dot(left, tok, NN)
        if image == 0:
            loads[2].wait()
        both = both + dot(right, out_v[image], NN)
        for k in range(slots // mine):
            sent_ref[k, image] = both[2 * mine * k : 2 * mine * (k + 1)].astype(jnp.bfloat16)
    loads[3].wait()
    loads[4].wait()


def route_forward(tokens, grad_out, param_t, weight_in, weight_out, owners):
    images, patches, width = tokens.shape
    slots = param_t.shape[0]
    mine = slots // owners
    first = first_columns(weight_in.shape[2])
    vmem = pl.BlockSpec(memory_space=pltpu.VMEM)
    hbm = pl.BlockSpec(memory_space=pl.ANY)
    return pl.pallas_call(
        lambda *refs: route_kernel(mine, *refs),
        in_specs=[hbm] * 5,
        out_specs=[vmem] * 4,
        out_shape=[
            jax.ShapeDtypeStruct((owners, images, 2 * mine, width), jnp.bfloat16),
            jax.ShapeDtypeStruct((images, 2 * slots, patches), jnp.float32),
            jax.ShapeDtypeStruct((width, first), jnp.bfloat16),
            jax.ShapeDtypeStruct((first, width), jnp.bfloat16),
        ],
        scratch_shapes=[
            pltpu.VMEM(tokens.shape, jnp.bfloat16),
            pltpu.VMEM(grad_out.shape, jnp.bfloat16),
            pltpu.VMEM(param_t.shape, jnp.bfloat16),
            pltpu.SemaphoreType.DMA((5,)),
        ],
        compiler_params=pltpu.CompilerParams(vmem_limit_bytes=16 << 20),
        name="route_forward",
    )(in_hbm(tokens), in_hbm(grad_out), in_hbm(param_t), in_hbm(weight_in), in_hbm(weight_out))


def route_back_kernel(mine, side_ref, back_ref, mix_ref, tok_ref, out_ref, rows_ref, dl_ref, keep_ref, give_ref, raw, part):
    slots = dl_ref.shape[1]
    total = None
    for image in range(tok_ref.shape[0]):
        for k in range(slots // mine):
            raw[2 * mine * k : 2 * mine * (k + 1), :] = back_ref[k, image].astype(jnp.float32)
        rows = raw[...].astype(jnp.bfloat16)
        rows_ref[image] = rows
        tok = tok_ref[image]
        mix = mix_ref[image]
        is_in = row_kind(mix.shape, mine) == 0
        d = jnp.where(is_in, dot(rows, tok, NT), dot(rows, out_ref[image], NT))
        weighed = mix * d
        over_patches = jnp.sum(weighed, axis=1, keepdims=True)
        over_slots = jnp.sum(jnp.where(is_in, 0.0, weighed), axis=0, keepdims=True)
        term = mix * (d - jnp.where(is_in, over_patches, over_slots))
        pair = (term + pltpu.roll(term, 2 * slots - mine, 0)).astype(jnp.bfloat16)
        dl = dot(slot_rows(slots, mine, False, 0), pair, NN).astype(jnp.bfloat16)
        dl_ref[image] = dl
        local = dot(dl, tok, NN)
        total = local if total is None else total + local
    half = slots // 2
    part[...] = total
    side = side_ref[0]
    keep_ref[...] = part[pl.ds(pl.multiple_of(side * half, half), half), :].astype(jnp.bfloat16)
    give_ref[...] = part[pl.ds(pl.multiple_of((1 - side) * half, half), half), :].astype(jnp.bfloat16)


def route_back(side, back, mix, tokens, grad_out):
    owners, images, block, width = back.shape
    mine = block // 2
    slots = owners * mine
    vmem = pl.BlockSpec(memory_space=pltpu.VMEM)
    return pl.pallas_call(
        lambda *refs: route_back_kernel(mine, *refs),
        in_specs=[pl.BlockSpec(memory_space=pltpu.SMEM)] + [vmem] * 4,
        out_specs=[vmem] * 4,
        out_shape=[
            jax.ShapeDtypeStruct((images, 2 * slots, width), jnp.bfloat16),
            jax.ShapeDtypeStruct((images, slots, tokens.shape[1]), jnp.bfloat16),
            jax.ShapeDtypeStruct((slots // 2, width), jnp.bfloat16),
            jax.ShapeDtypeStruct((slots // 2, width), jnp.bfloat16),
        ],
        scratch_shapes=[
            pltpu.VMEM((2 * slots, width), jnp.float32),
            pltpu.VMEM((slots, width), jnp.float32),
        ],
        compiler_params=pltpu.CompilerParams(vmem_limit_bytes=16 << 20),
        name="route_back",
    )(side, back, mix, tokens, grad_out)


def token_grad_kernel(mine, mix_ref, rows_ref, dl_ref, par_ref, grad_ref):
    mix = mix_ref[0]
    left = jnp.where(row_kind(mix.shape, mine) == 0, mix, 0.0).astype(jnp.bfloat16)
    grad_ref[0] = (dot(left, rows_ref[0], TN) + dot(dl_ref[0], par_ref[...], TN)).astype(jnp.bfloat16)


def token_grads(mine, mix, rows, dl, param_t):
    images, twice, patches = mix.shape
    slots, width = param_t.shape
    return pl.pallas_call(
        lambda *refs: token_grad_kernel(mine, *refs),
        grid=(images,),
        in_specs=[
            pl.BlockSpec((1, twice, patches), lambda i: (i, 0, 0)),
            pl.BlockSpec((1, twice, width), lambda i: (i, 0, 0)),
            pl.BlockSpec((1, slots, patches), lambda i: (i, 0, 0)),
            pl.BlockSpec((slots, width), lambda i: (0, 0)),
        ],
        out_specs=pl.BlockSpec((1, patches, width), lambda i: (i, 0, 0)),
        out_shape=jax.ShapeDtypeStruct((images, patches, width), jnp.bfloat16),
        compiler_params=pltpu.CompilerParams(vmem_limit_bytes=16 << 20),
        name="token_grads",
    )(mix, rows, dl, param_t)


def expert_body(
    experts, chunks, x_ref, first_in, first_out, win_hbm, wout_hbm,
    part_ref, give_ref, hid_ref, dpre_ref, win_v, wout_v, sems,
):
    own = part_ref.shape[1]
    step = win_v.shape[2] // chunks
    order = [(e, c) for e in range(experts) for c in range(chunks)]
    held = first_in.shape[1] // step

    def copies(k):
        e, c = order[k]
        cols = pl.ds(c * step, step)
        return (
            pltpu.make_async_copy(win_hbm.at[e, :, cols], win_v.at[e, :, cols], sems.at[0, e, c]),
            pltpu.make_async_copy(wout_hbm.at[e, cols, :], wout_v.at[e, cols, :], sems.at[1, e, c]),
        )

    def start(k):
        if k < len(order):
            for copy in copies(k):
                copy.start()

    def weights(k):
        e, c = order[k]
        cols = pl.ds(c * step, step)
        if k < held:
            return first_in.at[:, cols], first_out.at[cols, :]
        return win_v.at[e, :, cols], wout_v.at[e, cols, :]

    groups = {held: 1}
    k = held + 1
    while k < len(order):
        groups[k] = min(2, len(order) - k)
        k += groups[k]

    for k in range(held, held + FLIGHT):
        start(k)
    ready = out = grad = None
    for k in range(len(order) + 1):
        for arriving in range(k, k + groups.get(k, 0)):
            if arriving < len(order):
                for copy in copies(arriving):
                    copy.wait()
                start(arriving + FLIGHT)
        before = ready
        if k < len(order):
            w1, w2 = weights(k)
            e = order[k][0]
            ready = dot(x_ref[e], w1[...], NN), dot(x_ref[experts + e], w2[...], NT)
        if before is None:
            continue
        e, c = order[k - 1]
        w1, w2 = weights(k - 1)
        cols = pl.ds(c * step, step)
        pre, back = before
        value, slope = gelu_parts(pre)
        hidden = value.astype(jnp.bfloat16)
        dpre = (back * slope).astype(jnp.bfloat16)
        hid_ref[e, :, cols] = hidden
        dpre_ref[e, :, cols] = dpre
        o = dot(hidden, w2[...], NN)
        d = dot(dpre, w1[...], NT)
        out, grad = (o, d) if c == 0 else (out + o, grad + d)
        if c == chunks - 1:
            part_ref[e] = grad[:own]
            part_ref[experts + e] = out[:own]
            if own < out.shape[0]:
                give_ref[e] = grad[own:].astype(jnp.bfloat16)
                give_ref[experts + e] = out[own:].astype(jnp.bfloat16)
            else:
                give_ref[...] = jnp.zeros_like(give_ref)


def expert_forward(rows_in, first_in, first_out, weight_in, weight_out, own):
    experts, width, hid = weight_in.shape
    rows = rows_in.shape[1]
    chunks = chunk_count(hid, CHUNKS)
    vmem = pl.BlockSpec(memory_space=pltpu.VMEM)
    hbm = pl.BlockSpec(memory_space=pl.ANY)
    return pl.pallas_call(
        lambda *refs: expert_body(experts, chunks, *refs),
        in_specs=[vmem, vmem, vmem, hbm, hbm],
        out_specs=[vmem, vmem, vmem, vmem],
        out_shape=[
            jax.ShapeDtypeStruct((2 * experts, own, width), jnp.float32),
            jax.ShapeDtypeStruct((2 * experts, max(rows - own, 8), width), jnp.bfloat16),
            jax.ShapeDtypeStruct((experts, rows, hid), jnp.bfloat16),
            jax.ShapeDtypeStruct((experts, rows, hid), jnp.bfloat16),
        ],
        scratch_shapes=[
            pltpu.VMEM((experts, width, hid), jnp.bfloat16),
            pltpu.VMEM((experts, hid, width), jnp.bfloat16),
            pltpu.SemaphoreType.DMA((2, experts, chunks)),
        ],
        compiler_params=pltpu.CompilerParams(vmem_limit_bytes=22 << 20),
        name="expert_forward",
    )(rows_in, first_in, first_out, in_hbm(weight_in), in_hbm(weight_out))


def weight_grad_kernel(x_ref, g_ref, hid_ref, dpre_ref, gin_ref, gout_ref):
    gin_ref[0] = dot(x_ref[0], dpre_ref[0], TN).astype(jnp.bfloat16)
    gout_ref[0] = dot(hid_ref[0], g_ref[0], TN).astype(jnp.bfloat16)


def weight_grads(rows_in, hidden, dpre):
    experts, rows, hid = hidden.shape
    width = rows_in.shape[2]
    chunks = chunk_count(hid, 4)
    step = hid // chunks
    return pl.pallas_call(
        weight_grad_kernel,
        grid=(experts, chunks),
        in_specs=[
            pl.BlockSpec((1, rows, width), lambda e, c: (e, 0, 0)),
            pl.BlockSpec((1, rows, width), lambda e, c: (experts + e, 0, 0)),
            pl.BlockSpec((1, rows, step), lambda e, c: (e, 0, c)),
            pl.BlockSpec((1, rows, step), lambda e, c: (e, 0, c)),
        ],
        out_specs=[
            pl.BlockSpec((1, width, step), lambda e, c: (e, 0, c)),
            pl.BlockSpec((1, step, width), lambda e, c: (e, c, 0)),
        ],
        out_shape=[
            jax.ShapeDtypeStruct((experts, width, hid), jnp.bfloat16),
            jax.ShapeDtypeStruct((experts, hid, width), jnp.bfloat16),
        ],
        compiler_params=pltpu.CompilerParams(vmem_limit_bytes=24 << 20),
        name="weight_grads",
    )(rows_in, rows_in, hidden, dpre)


def swap(value, axis, mask):
    size = lax.axis_size(axis)
    return lax.ppermute(value, axis, [(k, k ^ mask) for k in range(size)])


def is_pow2(n):
    return n & (n - 1) == 0


def sum_bits(acc, axis, first_bit):
    size = lax.axis_size(axis)
    bit = first_bit
    while bit < size:
        sent = acc.astype(jnp.bfloat16)
        own = sent.astype(jnp.float32)
        if 2 * bit < size:
            a, b, c = (swap(sent, axis, m).astype(jnp.float32) for m in (bit, 2 * bit, 3 * bit))
            acc = (own + a) + (b + c)
            bit *= 4
        else:
            acc = own + swap(sent, axis, bit).astype(jnp.float32)
            bit *= 2
    return acc


def sum_everywhere(keep, give, side):
    ex, ey = lax.axis_size("ex"), lax.axis_size("ey")
    if not (is_pow2(ex) and is_pow2(ey)):
        low = jnp.where(side == 0, keep, give).astype(jnp.float32)
        high = jnp.where(side == 0, give, keep).astype(jnp.float32)
        return lax.psum(jnp.concatenate((low, high), axis=0), ("ex", "ey"))
    acc = keep.astype(jnp.float32) + swap(give, "ex", 1).astype(jnp.float32)
    acc = sum_bits(acc, "ex", 2)
    acc = sum_bits(acc, "ey", 1)
    sent = acc.astype(jnp.bfloat16)
    own = sent.astype(jnp.float32)
    other = swap(sent, "ex", 1)
    other = other.astype(jnp.float32)
    return jnp.concatenate((jnp.where(side == 0, own, other), jnp.where(side == 0, other, own)), axis=0)


def gather_ex(value):
    if lax.axis_size("ex") == 2:
        return jnp.stack((value, swap(value, "ex", 1)))
    return lax.all_gather(value, "ex", axis=0)


def join_kernel(keep_ref, got_ref, sum_hbm, sum_v, sem):
    block, rows, width = keep_ref.shape
    total = (keep_ref[...] + got_ref[...].astype(jnp.float32)).reshape(block * rows, width)
    shape = (block * rows, block * rows)
    to = lax.broadcasted_iota(jnp.int32, shape, 0)
    at = lax.broadcasted_iota(jnp.int32, shape, 1)
    move = jnp.where((to % block) * rows + to // block == at, 1.0, 0.0).astype(jnp.bfloat16)
    moved = dot(move, total.astype(jnp.bfloat16), NN)
    for k in range(rows):
        sum_v[k] = moved[block * k : block * (k + 1)].astype(jnp.bfloat16)
    copy = pltpu.make_async_copy(sum_v, sum_hbm, sem)
    copy.start()
    copy.wait()


def join(keep, got):
    block, rows, width = keep.shape
    vmem = pl.BlockSpec(memory_space=pltpu.VMEM)
    return pl.pallas_call(
        lambda *refs: join_kernel(*refs),
        in_specs=[vmem, vmem],
        out_specs=pl.BlockSpec(memory_space=pl.ANY),
        out_shape=pltpu.HBM((rows, block, width), jnp.bfloat16),
        scratch_shapes=[pltpu.VMEM((rows, block, width), jnp.bfloat16), pltpu.SemaphoreType.DMA],
        compiler_params=pltpu.CompilerParams(vmem_limit_bytes=16 << 20),
        name="join",
    )(keep, got)


def per_device(tokens, slot_param, weight_in, weight_out, grad_out):
    ex, ey = lax.axis_size("ex"), lax.axis_size("ey")
    images, _, width = tokens.shape
    slots = slot_param.shape[1]
    mine = slots // ey
    param_t = slot_param.T
    sent, mix, first_in, first_out = route_forward(tokens, grad_out, param_t, weight_in, weight_out, ey)
    moved = lax.all_to_all(sent.reshape(ey * images, 2 * mine, width), "ey", split_axis=0, concat_axis=0, tiled=True)
    arrived = gather_ex(moved)
    rows = ex * ey * images
    rows_in = arrived.reshape(rows, 2 * mine, width).transpose(1, 0, 2)
    own = rows // 2 if ex == 2 else rows
    keep_rows, give_rows, hidden, dpre = expert_forward(
        rows_in, first_in, first_out, weight_in, weight_out, own
    )
    if ex == 2:
        summed = join(keep_rows, swap(give_rows, "ex", 1))
    else:
        blocks = keep_rows.astype(jnp.bfloat16).transpose(1, 0, 2).reshape(ex, ey * images, 2 * mine, width)
        summed = lax.psum_scatter(blocks, "ex", scatter_dimension=0)
    back = lax.all_to_all(summed, "ey", split_axis=0, concat_axis=0, tiled=True)
    grad_win, grad_wout = weight_grads(rows_in, hidden, dpre)
    side = lax.axis_index("ex") % 2
    back_rows, logit_grad, keep, give = route_back(
        side.reshape(1), back.reshape(ey, images, 2 * mine, width), mix, tokens, grad_out
    )
    grad_param = sum_everywhere(keep, give, side).T
    grad_tokens = token_grads(mine, mix, back_rows, logit_grad, param_t)
    return (grad_tokens, grad_param, grad_win, grad_wout)


def solution(mesh):
    in_specs = (
        P(("ex", "ey"), None, None),
        P(),
        P("ey", None, "ex"),
        P("ey", "ex", None),
        P(("ex", "ey"), None, None),
    )
    out_specs = (P(("ex", "ey"), None, None), P(), P("ey", None, "ex"), P("ey", "ex", None))

    return jax.shard_map(per_device, mesh=mesh, in_specs=in_specs, out_specs=out_specs, check_vma=False)
```

time: 67.7 us -> 68.7 us (1.015)
  waiting for transfers between devices: 13.8 us -> 16.9 us
  matrix products: 2.28 us -> 0 us
  Pallas kernels: 20.5 us -> 21.9 us
  local copies, waits for them, and re-layouts: 1.22 us -> 0.1 us
    ppermute x10, waiting for transfers between devices: 5.8 us -> 8.92 us  [swap(): return lax.ppermute(value, axis, [(k, k ^ mask) for k in range(size)])]
    pallas_call x1 -> x4, Pallas kernels: 2.13 us -> 5.22 us  [the longest x1 2.3 us: route_forward(): pl.pallas_call(lambda *refs: route_kernel(mine, *refs), in_specs=[hbm] *...]
    dot_general x5 -> x0, matrix products: 2.28 us -> none  [the longest x1 1.11 us: per_device(): jnp.einsum('isp,sd->ipd', logit_grad, param_t, preferred_element_type=jnp...]
    pallas_call x1, Pallas kernels: 10.6 us -> 8.79 us  [expert_forward(): pl.pallas_call(lambda *refs: expert_body(experts, chunks, *refs), in_spec...]
    convert_element_type x1 -> x0, local copies, waits for them, and re-layouts: 0.76 us -> none  [scatter_sum_ex(): return (parts[0] + got.astype(jnp.float32)).astype(jnp.bfloat16)]
  transfers between devices with their start and end apart: 11 -> 11, of which waited for: 7 -> 9; matrix products, arithmetic and copies ran while one was open for 2% -> 0% of each run, Pallas kernels for 12% -> 13%
where the time goes in v1:
time: 68.7 us; the launch traced here: 68.4 us
  Pallas kernels  21.9 us (32%)
  waiting for transfers between devices  16.9 us (25%)
  blocking collectives  15.9 us (23%)
  starting transfers between devices  11.9 us (17%)
  other arithmetic  0.91 us (1%)
  between operations  0.76 us (1%)
    all_to_all x1, blocking collectives, per_device(): lax.all_to_all(sent.reshape(ey * images, 2 * mine, width), 'ey', split_ax...  15.9 us
    ppermute x10, waiting for transfers between devices, swap(): return lax.ppermute(value, axis, [(k, k ^ mask) for k in range(size)])  8.92 us
    pallas_call x1, Pallas kernels, expert_forward(): pl.pallas_call(lambda *refs: expert_body(experts, chunks, *refs), in_spec...  8.79 us
    ppermute x10, starting transfers between devices, swap(): return lax.ppermute(value, axis, [(k, k ^ mask) for k in range(size)])  8.36 us
    all_to_all x1, waiting for transfers between devices, per_device(): back = lax.all_to_all(summed, 'ey', split_axis=0, concat_axis=0, tiled=True)  7.99 us
    pallas_call x1, Pallas kernels, weight_grads(): pl.pallas_call(weight_grad_kernel, grid=(experts, chunks), in_specs=[pl.B...  7.84 us
    all_to_all x1, starting transfers between devices, per_device(): back = lax.all_to_all(summed, 'ey', split_axis=0, concat_axis=0, tiled=True)  3.52 us
    pallas_call x1, Pallas kernels, route_forward(): pl.pallas_call(lambda *refs: route_kernel(mine, *refs), in_specs=[hbm] *...  2.3 us
  transfers between devices with their start and end apart: 11, of which 9 were waited for; matrix products, arithmetic and copies ran while one was open for 0% of the time, Pallas kernels for 13%

profile of v1, /device:TPU:0, one launch (start us, length us, event | category | flops | bytes accessed | tf_op | source)
XLA Modules:
  0.0 68.4 jit_solution(12966833679748433940)
XLA Ops:
  0.6 2.3 %route_forward.1 = (bf16[16,1,4,1024]{3,2,1,0:T(4,128)(2,1)S(1)}, f32[1,64,256]{2,1,0:T(8,128)S(1)}, bf16[1024,768]{1,0:T(8,128)(2,1)S(1)}, bf16[768,1024]{1,0:T(8,128)(2,1)S(1)}) custom-call(bf16[1,256,1024]{2,1,0:T(8,128)(2,1)} %refs_3_.5, bf16[1,256,1024]{2,1,0:T(8,128)(2,1)} %refs_4_.5, bf16[32,1024]{1,0:T(8,128)(2,1)} %bitcast.15, ...), custom_call_target="tpu_custom_call" | custom-call | tf_op jit(solution)/shard_map/route_forward/pallas_call | solution.py:104
  2.9 15.9 %all_to_all.10 = bf16[16,4,1024]{2,1,0:T(4,128)(2,1)S(1)} all-to-all(bf16[16,4,1024]{2,1,0:T(4,128)(2,1)S(1)} %bitcast.17), channel_id=1, replica_groups=mesh['ex'=2,'ey'=16] {'ey'}, dimensions={0} | all-to-all | bytes 262144 | tf_op jit(solution)/shard_map/all_to_all | solution.py:416
  18.9 1.3 %collective-permute-done = bf16[16,4,1024]{2,1,0:T(4,128)(2,1)S(1)} collective-permute-done((bf16[16,4,1024]{2,1,0:T(4,128)(2,1)S(1)}, bf16[16,4,1024]{2,1,0:T(4,128)(2,1)S(1)}, u32[]{:S(2)}, u32[]{:S(2)}) %collective-permute-start) | collective-permute-done | bytes 131104 | tf_op jit(solution)/shard_map/ppermute | solution.py:335
  20.5 8.8 %expert_forward.1 = (f32[4,16,1024]{2,1,0:T(8,128)S(1)}, bf16[4,16,1024]{2,1,0:T(8,128)(2,1)S(1)}, bf16[2,32,2048]{2,1,0:T(8,128)(2,1)S(1)}, bf16[2,32,2048]{2,1,0:T(8,128)(2,1)S(1)}) custom-call(bf16[4,32,1024]{2,1,0:T(8,128)(2,1)S(1)} %bitcast.11, bf16[1024,768]{1,0:T(8,128)(2,1)S(1)} %get-tuple-element.20.refs_1_, ...), custom_call_target="tpu_custom_call" | custom-call | tf_op jit(solution)/shard_map/expert_forward/pallas_call | solution.py:281
  29.3 0.2 collective-permute-start.1
  29.5 1.2 %collective-permute-done.1.refs_1_ = bf16[4,16,1024]{2,1,0:T(8,128)(2,1)S(1)} collective-permute-done((bf16[4,16,1024]{2,1,0:T(8,128)(2,1)S(1)}, bf16[4,16,1024]{2,1,0:T(8,128)(2,1)S(1)}, u32[]{:S(2)}, u32[]{:S(2)}) %collective-permute-start.1) | collective-permute-done | bytes 131104 | tf_op jit(solution)/shard_map/ppermute | solution.py:335
  30.7 0.8 %join.1 = bf16[16,4,1024]{2,1,0:T(4,128)(2,1)} custom-call(f32[4,16,1024]{2,1,0:T(8,128)S(1)} %get-tuple-element.22.refs_0_, bf16[4,16,1024]{2,1,0:T(8,128)(2,1)S(1)} %collective-permute-done.1.refs_1_), custom_call_target="tpu_custom_call" | custom-call | tf_op jit(solution)/shard_map/join/pallas_call | solution.py:398
  31.6 3.5 %all-to-all-start.1 = ((bf16[16,4,1024]{2,1,0:T(4,128)(2,1)}), bf16[16,4,1024]{2,1,0:T(4,128)(2,1)S(1)}, u32[]{:S(2)}, u32[]{:S(2)}) async-start(bf16[16,4,1024]{2,1,0:T(4,128)(2,1)} %join.1), calls=%async_computation.1 | async-start | bytes 262144 | tf_op jit(solution)/shard_map/all_to_all | solution.py:429
  35.1 8.0 %all-to-all-done.1 = bf16[16,4,1024]{2,1,0:T(4,128)(2,1)S(1)} async-done(((bf16[16,4,1024]{2,1,0:T(4,128)(2,1)}), bf16[16,4,1024]{2,1,0:T(4,128)(2,1)S(1)}, u32[]{:S(2)}, u32[]{:S(2)}) %all-to-all-start.1) | async-done | bytes 131104 | tf_op jit(solution)/shard_map/all_to_all | solution.py:429
  43.1 0.8 %route_back.1 = (bf16[1,64,1024]{2,1,0:T(8,128)(2,1)S(1)}, bf16[1,32,256]{2,1,0:T(8,128)(2,1)S(1)}, bf16[16,1024]{1,0:T(8,128)(2,1)S(1)}, bf16[16,1024]{1,0:T(8,128)(2,1)S(1)}) custom-call(s32[1]{0:T(128)} %bitcast.1.refs_0_, bf16[16,1,4,1024]{3,2,1,0:T(4,128)(2,1)S(1)} %bitcast.14, f32[1,64,256]{2,1,0:T(8,128)S(1)} %get-tuple-element.18.refs_2_.refs_0_, ...), custom_call_target="tpu_custom_call" | custom-call | tf_op jit(solution)/shard_map/route_back/pallas_call | solution.py:158
  44.1 1.2 %collective-permute-done.2 = bf16[16,1024]{1,0:T(8,128)(2,1)S(1)} collective-permute-done((bf16[16,1024]{1,0:T(8,128)(2,1)S(1)}, bf16[16,1024]{1,0:T(8,128)(2,1)S(1)}, u32[]{:S(2)}, u32[]{:S(2)}) %collective-permute-start.2) | collective-permute-done | bytes 32800 | tf_op jit(solution)/shard_map/ppermute | solution.py:335
  45.3 0.8 %collective-permute-start.5 = (bf16[16,1024]{1,0:T(8,128)(2,1)S(1)}, bf16[16,1024]{1,0:T(8,128)(2,1)S(1)}, u32[]{:S(2)}, u32[]{:S(2)}) collective-permute-start(bf16[16,1024]{1,0:T(8,128)(2,1)S(1)} %add_convert_fusion.2), channel_id=1, source_target_pairs={{0,3},{1,2},{2,1},{3,0},{4,7},{5,6},{6,5},{7,4},{8,11},{9,10},{10,... | collective-permute-start | bytes 98312 | tf_op jit(solution)/shard_map/ppermute | solution.py:335
  46.1 1.8 %collective-permute-start.4 = (bf16[16,1024]{1,0:T(8,128)(2,1)S(1)}, bf16[16,1024]{1,0:T(8,128)(2,1)S(1)}, u32[]{:S(2)}, u32[]{:S(2)}) collective-permute-start(bf16[16,1024]{1,0:T(8,128)(2,1)S(1)} %add_convert_fusion.2), channel_id=1, source_target_pairs={{0,2},{1,3},{2,0},{3,1},{4,6},{5,7},{6,4},{7,5},{8,10},{9,11},{10,... | collective-permute-start | bytes 98312 | tf_op jit(solution)/shard_map/ppermute | solution.py:335
  47.9 0.9 %collective-permute-start.3 = (bf16[16,1024]{1,0:T(8,128)(2,1)S(1)}, bf16[16,1024]{1,0:T(8,128)(2,1)S(1)}, u32[]{:S(2)}, u32[]{:S(2)}) collective-permute-start(bf16[16,1024]{1,0:T(8,128)(2,1)S(1)} %add_convert_fusion.2), channel_id=1, source_target_pairs={{0,1},{1,0},{2,3},{3,2},{4,5},{5,4},{6,7},{7,6},{8,9},{9,8},{10,11... | collective-permute-start | bytes 98312 | tf_op jit(solution)/shard_map/ppermute | solution.py:335
  48.8 1.7 %collective-permute-done.5 = bf16[16,1024]{1,0:T(8,128)(2,1)S(1)} collective-permute-done((bf16[16,1024]{1,0:T(8,128)(2,1)S(1)}, bf16[16,1024]{1,0:T(8,128)(2,1)S(1)}, u32[]{:S(2)}, u32[]{:S(2)}) %collective-permute-start.5) | collective-permute-done | bytes 32800 | tf_op jit(solution)/shard_map/ppermute | solution.py:335
  50.5 1.3 %collective-permute-done.3 = bf16[16,1024]{1,0:T(8,128)(2,1)S(1)} collective-permute-done((bf16[16,1024]{1,0:T(8,128)(2,1)S(1)}, bf16[16,1024]{1,0:T(8,128)(2,1)S(1)}, u32[]{:S(2)}, u32[]{:S(2)}) %collective-permute-start.3) | collective-permute-done | bytes 32800 | tf_op jit(solution)/shard_map/ppermute | solution.py:335
  51.8 1.1 %collective-permute-start.8 = (bf16[16,1024]{1,0:T(8,128)(2,1)S(1)}, bf16[16,1024]{1,0:T(8,128)(2,1)S(1)}, u32[]{:S(2)}, u32[]{:S(2)}) collective-permute-start(bf16[16,1024]{1,0:T(8,128)(2,1)S(1)} %add_convert_fusion.1), channel_id=1, source_target_pairs={{0,12},{1,13},{2,14},{3,15},{4,8},{5,9},{6,10},{7,11},{8,4},{9,5},... | collective-permute-start | bytes 98312 | tf_op jit(solution)/shard_map/ppermute | solution.py:335
  52.9 0.6 collective-permute-start.7
  53.6 2.7 %collective-permute-start.6 = (bf16[16,1024]{1,0:T(8,128)(2,1)S(1)}, bf16[16,1024]{1,0:T(8,128)(2,1)S(1)}, u32[]{:S(2)}, u32[]{:S(2)}) collective-permute-start(bf16[16,1024]{1,0:T(8,128)(2,1)S(1)} %add_convert_fusion.1), channel_id=1, source_target_pairs={{0,4},{1,5},{2,6},{3,7},{4,0},{5,1},{6,2},{7,3},{8,12},{9,13},{10,... | collective-permute-start | bytes 98312 | tf_op jit(solution)/shard_map/ppermute | solution.py:335
  56.3 1.3 %collective-permute-done.8 = bf16[16,1024]{1,0:T(8,128)(2,1)S(1)} collective-permute-done((bf16[16,1024]{1,0:T(8,128)(2,1)S(1)}, bf16[16,1024]{1,0:T(8,128)(2,1)S(1)}, u32[]{:S(2)}, u32[]{:S(2)}) %collective-permute-start.8) | collective-permute-done | bytes 32800 | tf_op jit(solution)/shard_map/ppermute | solution.py:335
  57.6 0.8 %collective-permute-done.7 = bf16[16,1024]{1,0:T(8,128)(2,1)S(1)} collective-permute-done((bf16[16,1024]{1,0:T(8,128)(2,1)S(1)}, bf16[16,1024]{1,0:T(8,128)(2,1)S(1)}, u32[]{:S(2)}, u32[]{:S(2)}) %collective-permute-start.7) | collective-permute-done | bytes 32800 | tf_op jit(solution)/shard_map/ppermute | solution.py:335
  58.6 7.8 %weight_grads.1 = (bf16[2,1024,2048]{2,1,0:T(8,128)(2,1)}, bf16[2,2048,1024]{2,1,0:T(8,128)(2,1)}) custom-call(bf16[4,32,1024]{2,1,0:T(8,128)(2,1)S(1)} %bitcast.12, bf16[4,32,1024]{2,1,0:T(8,128)(2,1)S(1)} %bitcast.13, bf16[2,32,2048]{2,1,0:T(8,128)(2,1)S(1)} %get-tuple-element.28.hid_ref, bf16[2,32,2048]{2,1,0:T(8,128)(2,1)S(1)} %get-tuple-element.29.dpre_ref), custom_call_target="tpu_custom_call" | custom-call | tf_op jit(solution)/shard_map/weight_grads/pallas_call | solution.py:311
  66.4 1.2 %token_grads.1 = bf16[1,256,1024]{2,1,0:T(8,128)(2,1)} custom-call(f32[1,64,256]{2,1,0:T(8,128)S(1)} %get-tuple-element.18.refs_2_.refs_0_, bf16[1,64,1024]{2,1,0:T(8,128)(2,1)S(1)} %get-tuple-element.24.refs_1_, bf16[1,32,256]{2,1,0:T(8,128)(2,1)S(1)} %get-tuple-element.25.refs_2_, bf16[32,1024]{1,0:T(8,128)(2,1)S(1)} %bitcast.16), custom_call_target="tpu_custom_call" | custom-call | tf_op jit(solution)/shard_map/token_grads/pallas_call | solution.py:186
  67.7 0.7 maximum_bitcast_fusion
  (18 shorter events, 0.6 us)
Async XLA Ops:
  18.9 1.3 %collective-permute-start = (bf16[16,4,1024]{2,1,0:T(4,128)(2,1)S(1)}, bf16[16,4,1024]{2,1,0:T(4,128)(2,1)S(1)}, u32[]{:S(2)}, u32[]{:S(2)}) collective-permute-start(bf16[16,4,1024]{2,1,0:T(4,128)(2,1)S(1)} %all_to_all.10), channel_id=1, source_target_pairs={{0,16},{16,0},{1,17},{17,1},{2,18},{18,2},{3,19},{19,3},{4,20},{20... | collective-permute-start | bytes 393224 | tf_op jit(solution)/shard_map/ppermute | solution.py:335
  20.5 22.6 %copy-start = (bf16[1,256,1024]{2,1,0:T(8,128)(2,1)S(1)}, bf16[1,256,1024]{2,1,0:T(8,128)(2,1)}, u32[]{:S(2)}) copy-start(bf16[1,256,1024]{2,1,0:T(8,128)(2,1)} %refs_3_.5) | copy-start | bytes 1572868
  20.5 22.6 %copy-start.1 = (bf16[1,256,1024]{2,1,0:T(8,128)(2,1)S(1)}, bf16[1,256,1024]{2,1,0:T(8,128)(2,1)}, u32[]{:S(2)}) copy-start(bf16[1,256,1024]{2,1,0:T(8,128)(2,1)} %refs_4_.5) | copy-start | bytes 1572868
  20.5 45.9 %copy-start.2 = (bf16[1024,32]{0,1:T(8,128)(2,1)S(1)}, bf16[1024,32]{0,1:T(8,128)(2,1)}, u32[]{:S(2)}) copy-start(bf16[1024,32]{0,1:T(8,128)(2,1)} %param.6) | copy-start | bytes 196612
  29.3 1.4 %collective-permute-start.1 = (bf16[4,16,1024]{2,1,0:T(8,128)(2,1)S(1)}, bf16[4,16,1024]{2,1,0:T(8,128)(2,1)S(1)}, u32[]{:S(2)}, u32[]{:S(2)}) collective-permute-start(bf16[4,16,1024]{2,1,0:T(8,128)(2,1)S(1)} %get-tuple-element.23), channel_id=1, source_target_pairs={{0,16},{16,0},{1,17},{17,1},{2,18},{18,2},{3,19},{19,3},{4,20},{20... | collective-permute-start | bytes 393224 | tf_op jit(solution)/shard_map/ppermute | solution.py:335
  31.6 11.5 %all-to-all-start.1 = ((bf16[16,4,1024]{2,1,0:T(4,128)(2,1)}), bf16[16,4,1024]{2,1,0:T(4,128)(2,1)S(1)}, u32[]{:S(2)}, u32[]{:S(2)}) async-start(bf16[16,4,1024]{2,1,0:T(4,128)(2,1)} %join.1), calls=%async_computation.1 | async-start | bytes 262144 | tf_op jit(solution)/shard_map/all_to_all | solution.py:429
  44.0 1.3 %collective-permute-start.2 = (bf16[16,1024]{1,0:T(8,128)(2,1)S(1)}, bf16[16,1024]{1,0:T(8,128)(2,1)S(1)}, u32[]{:S(2)}, u32[]{:S(2)}) collective-permute-start(bf16[16,1024]{1,0:T(8,128)(2,1)S(1)} %get-tuple-element.27), channel_id=1, source_target_pairs={{0,16},{16,0},{1,17},{17,1},{2,18},{18,2},{3,19},{19,3},{4,20},{20... | collective-permute-start | bytes 98312 | tf_op jit(solution)/shard_map/ppermute | solution.py:335
  45.3 5.2 %collective-permute-start.5 = (bf16[16,1024]{1,0:T(8,128)(2,1)S(1)}, bf16[16,1024]{1,0:T(8,128)(2,1)S(1)}, u32[]{:S(2)}, u32[]{:S(2)}) collective-permute-start(bf16[16,1024]{1,0:T(8,128)(2,1)S(1)} %add_convert_fusion.2), channel_id=1, source_target_pairs={{0,3},{1,2},{2,1},{3,0},{4,7},{5,6},{6,5},{7,4},{8,11},{9,10},{10,... | collective-permute-start | bytes 98312 | tf_op jit(solution)/shard_map/ppermute | solution.py:335
  46.1 4.4 %collective-permute-start.4 = (bf16[16,1024]{1,0:T(8,128)(2,1)S(1)}, bf16[16,1024]{1,0:T(8,128)(2,1)S(1)}, u32[]{:S(2)}, u32[]{:S(2)}) collective-permute-start(bf16[16,1024]{1,0:T(8,128)(2,1)S(1)} %add_convert_fusion.2), channel_id=1, source_target_pairs={{0,2},{1,3},{2,0},{3,1},{4,6},{5,7},{6,4},{7,5},{8,10},{9,11},{10,... | collective-permute-start | bytes 98312 | tf_op jit(solution)/shard_map/ppermute | solution.py:335
  47.9 3.9 %collective-permute-start.3 = (bf16[16,1024]{1,0:T(8,128)(2,1)S(1)}, bf16[16,1024]{1,0:T(8,128)(2,1)S(1)}, u32[]{:S(2)}, u32[]{:S(2)}) collective-permute-start(bf16[16,1024]{1,0:T(8,128)(2,1)S(1)} %add_convert_fusion.2), channel_id=1, source_target_pairs={{0,1},{1,0},{2,3},{3,2},{4,5},{5,4},{6,7},{7,6},{8,9},{9,8},{10,11... | collective-permute-start | bytes 98312 | tf_op jit(solution)/shard_map/ppermute | solution.py:335
  51.8 5.8 %collective-permute-start.8 = (bf16[16,1024]{1,0:T(8,128)(2,1)S(1)}, bf16[16,1024]{1,0:T(8,128)(2,1)S(1)}, u32[]{:S(2)}, u32[]{:S(2)}) collective-permute-start(bf16[16,1024]{1,0:T(8,128)(2,1)S(1)} %add_convert_fusion.1), channel_id=1, source_target_pairs={{0,12},{1,13},{2,14},{3,15},{4,8},{5,9},{6,10},{7,11},{8,4},{9,5},... | collective-permute-start | bytes 98312 | tf_op jit(solution)/shard_map/ppermute | solution.py:335
  52.9 5.5 %collective-permute-start.7 = (bf16[16,1024]{1,0:T(8,128)(2,1)S(1)}, bf16[16,1024]{1,0:T(8,128)(2,1)S(1)}, u32[]{:S(2)}, u32[]{:S(2)}) collective-permute-start(bf16[16,1024]{1,0:T(8,128)(2,1)S(1)} %add_convert_fusion.1), channel_id=1, source_target_pairs={{0,8},{1,9},{2,10},{3,11},{4,12},{5,13},{6,14},{7,15},{8,0},{9,1},... | collective-permute-start | bytes 98312 | tf_op jit(solution)/shard_map/ppermute | solution.py:335
  53.6 4.9 %collective-permute-start.6 = (bf16[16,1024]{1,0:T(8,128)(2,1)S(1)}, bf16[16,1024]{1,0:T(8,128)(2,1)S(1)}, u32[]{:S(2)}, u32[]{:S(2)}) collective-permute-start(bf16[16,1024]{1,0:T(8,128)(2,1)S(1)} %add_convert_fusion.1), channel_id=1, source_target_pairs={{0,4},{1,5},{2,6},{3,7},{4,0},{5,1},{6,2},{7,3},{8,12},{9,13},{10,... | collective-permute-start | bytes 98312 | tf_op jit(solution)/shard_map/ppermute | solution.py:335
  58.5 9.2 %collective-permute-start.9 = (bf16[16,1024]{1,0:T(8,128)(2,1)S(1)}, bf16[16,1024]{1,0:T(8,128)(2,1)S(1)}, u32[]{:S(2)}, u32[]{:S(2)}) collective-permute-start(bf16[16,1024]{1,0:T(8,128)(2,1)S(1)} %add_convert_fusion), channel_id=1, source_target_pairs={{0,16},{16,0},{1,17},{17,1},{2,18},{18,2},{3,19},{19,3},{4,20},{20... | collective-permute-start | bytes 98312 | tf_op jit(solution)/shard_map/ppermute | solution.py:335

commit v2 on v1

--- a/solution.py
+++ b/solution.py
@@ -35,7 +35,7 @@
     return wanted
 
 
-CHUNKS, AHEAD, FLIGHT = 8, 3, 4
+CHUNKS, AHEAD, FLIGHT = 8, 3, 8
 
 
 def first_columns(hid):
@@ -201,7 +201,7 @@
 
 def expert_body(
     experts, chunks, x_ref, first_in, first_out, win_hbm, wout_hbm,
-    part_ref, give_ref, hid_ref, dpre_ref, win_v, wout_v, sems,
+    part_ref, give_ref, hid_ref, dpre_ref, win_v, wout_v, win_t, wout_t, sems,
 ):
     own = part_ref.shape[1]
     step = win_v.shape[2] // chunks
@@ -247,11 +247,13 @@
         if k < len(order):
             w1, w2 = weights(k)
             e = order[k][0]
-            ready = dot(x_ref[e], w1[...], NN), dot(x_ref[experts + e], w2[...], NT)
+            win_t[k] = w1[...].T
+            wout_t[k] = w2[...].T
+            ready = dot(x_ref[e], w1[...], NN), dot(x_ref[experts + e], wout_t[k], NN)
         if before is None:
             continue
         e, c = order[k - 1]
-        w1, w2 = weights(k - 1)
+        w2 = weights(k - 1)[1]
         cols = pl.ds(c * step, step)
         pre, back = before
         value, slope = gelu_parts(pre)
@@ -260,7 +262,7 @@
         hid_ref[e, :, cols] = hidden
         dpre_ref[e, :, cols] = dpre
         o = dot(hidden, w2[...], NN)
-        d = dot(dpre, w1[...], NT)
+        d = dot(dpre, win_t[k - 1], NN)
         out, grad = (o, d) if c == 0 else (out + o, grad + d)
         if c == chunks - 1:
             part_ref[e] = grad[:own]
@@ -291,9 +293,11 @@
         scratch_shapes=[
             pltpu.VMEM((experts, width, hid), jnp.bfloat16),
             pltpu.VMEM((experts, hid, width), jnp.bfloat16),
+            pltpu.VMEM((experts * chunks, hid // chunks, width), jnp.bfloat16),
+            pltpu.VMEM((experts * chunks, width, hid // chunks), jnp.bfloat16),
             pltpu.SemaphoreType.DMA((2, experts, chunks)),
         ],
-        compiler_params=pltpu.CompilerParams(vmem_limit_bytes=22 << 20),
+        compiler_params=pltpu.CompilerParams(vmem_limit_bytes=40 << 20),
         name="expert_forward",
     )(rows_in, first_in, first_out, in_hbm(weight_in), in_hbm(weight_out))
 

time: 68.7 us -> 66.5 us (0.968)
  Pallas kernels: 21.9 us -> 19.7 us
    pallas_call x1, Pallas kernels: 8.79 us -> 6.65 us  [expert_forward(): pl.pallas_call(lambda *refs: expert_body(experts, chunks, *refs), in_spec...]
  transfers between devices with their start and end apart: 11 -> 11, of which waited for: 9 -> 9; matrix products, arithmetic and copies ran while one was open for 0% -> 0% of each run, Pallas kernels for 13% -> 14%
where the time goes in v2:
time: 66.5 us; the launch traced here: 66.2 us
  Pallas kernels  19.7 us (30%)
  waiting for transfers between devices  16.9 us (25%)
  blocking collectives  15.9 us (24%)
  starting transfers between devices  11.9 us (18%)
  other arithmetic  0.91 us (1%)
  between operations  0.76 us (1%)
    all_to_all x1, blocking collectives, per_device(): lax.all_to_all(sent.reshape(ey * images, 2 * mine, width), 'ey', split_ax...  15.9 us
    ppermute x10, waiting for transfers between devices, swap(): return lax.ppermute(value, axis, [(k, k ^ mask) for k in range(size)])  8.92 us
    ppermute x10, starting transfers between devices, swap(): return lax.ppermute(value, axis, [(k, k ^ mask) for k in range(size)])  8.36 us
    all_to_all x1, waiting for transfers between devices, per_device(): back = lax.all_to_all(summed, 'ey', split_axis=0, concat_axis=0, tiled=True)  7.99 us
    pallas_call x1, Pallas kernels, weight_grads(): pl.pallas_call(weight_grad_kernel, grid=(experts, chunks), in_specs=[pl.B...  7.85 us
    pallas_call x1, Pallas kernels, expert_forward(): pl.pallas_call(lambda *refs: expert_body(experts, chunks, *refs), in_spec...  6.65 us
    all_to_all x1, starting transfers between devices, per_device(): back = lax.all_to_all(summed, 'ey', split_axis=0, concat_axis=0, tiled=True)  3.52 us
    pallas_call x1, Pallas kernels, route_forward(): pl.pallas_call(lambda *refs: route_kernel(mine, *refs), in_specs=[hbm] *...  2.3 us
  transfers between devices with their start and end apart: 11, of which 9 were waited for; matrix products, arithmetic and copies ran while one was open for 0% of the time, Pallas kernels for 14%

profile of v2, /device:TPU:0, one launch (start us, length us, event | category | flops | bytes accessed | tf_op | source)
XLA Modules:
  0.0 66.2 jit_solution(10254686205446647639)
XLA Ops:
  0.6 2.3 %route_forward.1 = (bf16[16,1,4,1024]{3,2,1,0:T(4,128)(2,1)S(1)}, f32[1,64,256]{2,1,0:T(8,128)S(1)}, bf16[1024,768]{1,0:T(8,128)(2,1)S(1)}, bf16[768,1024]{1,0:T(8,128)(2,1)S(1)}) custom-call(bf16[1,256,1024]{2,1,0:T(8,128)(2,1)} %refs_3_.5, bf16[1,256,1024]{2,1,0:T(8,128)(2,1)} %refs_4_.5, bf16[32,1024]{1,0:T(8,128)(2,1)} %bitcast.15, ...), custom_call_target="tpu_custom_call" | custom-call | tf_op jit(solution)/shard_map/route_forward/pallas_call | solution.py:104
  2.9 15.9 %all_to_all.10 = bf16[16,4,1024]{2,1,0:T(4,128)(2,1)S(1)} all-to-all(bf16[16,4,1024]{2,1,0:T(4,128)(2,1)S(1)} %bitcast.17), channel_id=1, replica_groups=mesh['ex'=2,'ey'=16] {'ey'}, dimensions={0} | all-to-all | bytes 262144 | tf_op jit(solution)/shard_map/all_to_all | solution.py:420
  18.9 1.3 %collective-permute-done = bf16[16,4,1024]{2,1,0:T(4,128)(2,1)S(1)} collective-permute-done((bf16[16,4,1024]{2,1,0:T(4,128)(2,1)S(1)}, bf16[16,4,1024]{2,1,0:T(4,128)(2,1)S(1)}, u32[]{:S(2)}, u32[]{:S(2)}) %collective-permute-start) | collective-permute-done | bytes 131104 | tf_op jit(solution)/shard_map/ppermute | solution.py:339
  20.5 6.6 %expert_forward.1 = (f32[4,16,1024]{2,1,0:T(8,128)S(1)}, bf16[4,16,1024]{2,1,0:T(8,128)(2,1)S(1)}, bf16[2,32,2048]{2,1,0:T(8,128)(2,1)S(1)}, bf16[2,32,2048]{2,1,0:T(8,128)(2,1)S(1)}) custom-call(bf16[4,32,1024]{2,1,0:T(8,128)(2,1)S(1)} %bitcast.11, bf16[1024,768]{1,0:T(8,128)(2,1)S(1)} %get-tuple-element.20.refs_1_, ...), custom_call_target="tpu_custom_call" | custom-call | tf_op jit(solution)/shard_map/expert_forward/pallas_call | solution.py:283
  27.2 0.2 collective-permute-start.1
  27.4 1.2 %collective-permute-done.1.refs_1_ = bf16[4,16,1024]{2,1,0:T(8,128)(2,1)S(1)} collective-permute-done((bf16[4,16,1024]{2,1,0:T(8,128)(2,1)S(1)}, bf16[4,16,1024]{2,1,0:T(8,128)(2,1)S(1)}, u32[]{:S(2)}, u32[]{:S(2)}) %collective-permute-start.1) | collective-permute-done | bytes 131104 | tf_op jit(solution)/shard_map/ppermute | solution.py:339
  28.6 0.8 %join.1 = bf16[16,4,1024]{2,1,0:T(4,128)(2,1)} custom-call(f32[4,16,1024]{2,1,0:T(8,128)S(1)} %get-tuple-element.22.refs_0_, bf16[4,16,1024]{2,1,0:T(8,128)(2,1)S(1)} %collective-permute-done.1.refs_1_), custom_call_target="tpu_custom_call" | custom-call | tf_op jit(solution)/shard_map/join/pallas_call | solution.py:402
  29.5 3.5 %all-to-all-start.1 = ((bf16[16,4,1024]{2,1,0:T(4,128)(2,1)}), bf16[16,4,1024]{2,1,0:T(4,128)(2,1)S(1)}, u32[]{:S(2)}, u32[]{:S(2)}) async-start(bf16[16,4,1024]{2,1,0:T(4,128)(2,1)} %join.1), calls=%async_computation.1 | async-start | bytes 262144 | tf_op jit(solution)/shard_map/all_to_all | solution.py:433
  33.0 8.0 %all-to-all-done.1 = bf16[16,4,1024]{2,1,0:T(4,128)(2,1)S(1)} async-done(((bf16[16,4,1024]{2,1,0:T(4,128)(2,1)}), bf16[16,4,1024]{2,1,0:T(4,128)(2,1)S(1)}, u32[]{:S(2)}, u32[]{:S(2)}) %all-to-all-start.1) | async-done | bytes 131104 | tf_op jit(solution)/shard_map/all_to_all | solution.py:433
  41.0 0.8 %route_back.1 = (bf16[1,64,1024]{2,1,0:T(8,128)(2,1)S(1)}, bf16[1,32,256]{2,1,0:T(8,128)(2,1)S(1)}, bf16[16,1024]{1,0:T(8,128)(2,1)S(1)}, bf16[16,1024]{1,0:T(8,128)(2,1)S(1)}) custom-call(s32[1]{0:T(128)} %bitcast.1.refs_0_, bf16[16,1,4,1024]{3,2,1,0:T(4,128)(2,1)S(1)} %bitcast.14, f32[1,64,256]{2,1,0:T(8,128)S(1)} %get-tuple-element.18.refs_2_.refs_0_, ...), custom_call_target="tpu_custom_call" | custom-call | tf_op jit(solution)/shard_map/route_back/pallas_call | solution.py:158
  41.9 1.2 %collective-permute-done.2 = bf16[16,1024]{1,0:T(8,128)(2,1)S(1)} collective-permute-done((bf16[16,1024]{1,0:T(8,128)(2,1)S(1)}, bf16[16,1024]{1,0:T(8,128)(2,1)S(1)}, u32[]{:S(2)}, u32[]{:S(2)}) %collective-permute-start.2) | collective-permute-done | bytes 32800 | tf_op jit(solution)/shard_map/ppermute | solution.py:339
  43.1 0.8 %collective-permute-start.5 = (bf16[16,1024]{1,0:T(8,128)(2,1)S(1)}, bf16[16,1024]{1,0:T(8,128)(2,1)S(1)}, u32[]{:S(2)}, u32[]{:S(2)}) collective-permute-start(bf16[16,1024]{1,0:T(8,128)(2,1)S(1)} %add_convert_fusion.2), channel_id=1, source_target_pairs={{0,3},{1,2},{2,1},{3,0},{4,7},{5,6},{6,5},{7,4},{8,11},{9,10},{10,... | collective-permute-start | bytes 98312 | tf_op jit(solution)/shard_map/ppermute | solution.py:339
  43.9 1.8 %collective-permute-start.4 = (bf16[16,1024]{1,0:T(8,128)(2,1)S(1)}, bf16[16,1024]{1,0:T(8,128)(2,1)S(1)}, u32[]{:S(2)}, u32[]{:S(2)}) collective-permute-start(bf16[16,1024]{1,0:T(8,128)(2,1)S(1)} %add_convert_fusion.2), channel_id=1, source_target_pairs={{0,2},{1,3},{2,0},{3,1},{4,6},{5,7},{6,4},{7,5},{8,10},{9,11},{10,... | collective-permute-start | bytes 98312 | tf_op jit(solution)/shard_map/ppermute | solution.py:339
  45.7 0.9 %collective-permute-start.3 = (bf16[16,1024]{1,0:T(8,128)(2,1)S(1)}, bf16[16,1024]{1,0:T(8,128)(2,1)S(1)}, u32[]{:S(2)}, u32[]{:S(2)}) collective-permute-start(bf16[16,1024]{1,0:T(8,128)(2,1)S(1)} %add_convert_fusion.2), channel_id=1, source_target_pairs={{0,1},{1,0},{2,3},{3,2},{4,5},{5,4},{6,7},{7,6},{8,9},{9,8},{10,11... | collective-permute-start | bytes 98312 | tf_op jit(solution)/shard_map/ppermute | solution.py:339
  46.7 1.7 %collective-permute-done.5 = bf16[16,1024]{1,0:T(8,128)(2,1)S(1)} collective-permute-done((bf16[16,1024]{1,0:T(8,128)(2,1)S(1)}, bf16[16,1024]{1,0:T(8,128)(2,1)S(1)}, u32[]{:S(2)}, u32[]{:S(2)}) %collective-permute-start.5) | collective-permute-done | bytes 32800 | tf_op jit(solution)/shard_map/ppermute | solution.py:339
  48.4 1.3 %collective-permute-done.3 = bf16[16,1024]{1,0:T(8,128)(2,1)S(1)} collective-permute-done((bf16[16,1024]{1,0:T(8,128)(2,1)S(1)}, bf16[16,1024]{1,0:T(8,128)(2,1)S(1)}, u32[]{:S(2)}, u32[]{:S(2)}) %collective-permute-start.3) | collective-permute-done | bytes 32800 | tf_op jit(solution)/shard_map/ppermute | solution.py:339
  49.7 1.1 %collective-permute-start.8 = (bf16[16,1024]{1,0:T(8,128)(2,1)S(1)}, bf16[16,1024]{1,0:T(8,128)(2,1)S(1)}, u32[]{:S(2)}, u32[]{:S(2)}) collective-permute-start(bf16[16,1024]{1,0:T(8,128)(2,1)S(1)} %add_convert_fusion.1), channel_id=1, source_target_pairs={{0,12},{1,13},{2,14},{3,15},{4,8},{5,9},{6,10},{7,11},{8,4},{9,5},... | collective-permute-start | bytes 98312 | tf_op jit(solution)/shard_map/ppermute | solution.py:339
  50.8 0.6 collective-permute-start.7
  51.4 2.7 %collective-permute-start.6 = (bf16[16,1024]{1,0:T(8,128)(2,1)S(1)}, bf16[16,1024]{1,0:T(8,128)(2,1)S(1)}, u32[]{:S(2)}, u32[]{:S(2)}) collective-permute-start(bf16[16,1024]{1,0:T(8,128)(2,1)S(1)} %add_convert_fusion.1), channel_id=1, source_target_pairs={{0,4},{1,5},{2,6},{3,7},{4,0},{5,1},{6,2},{7,3},{8,12},{9,13},{10,... | collective-permute-start | bytes 98312 | tf_op jit(solution)/shard_map/ppermute | solution.py:339
  54.1 1.3 %collective-permute-done.8 = bf16[16,1024]{1,0:T(8,128)(2,1)S(1)} collective-permute-done((bf16[16,1024]{1,0:T(8,128)(2,1)S(1)}, bf16[16,1024]{1,0:T(8,128)(2,1)S(1)}, u32[]{:S(2)}, u32[]{:S(2)}) %collective-permute-start.8) | collective-permute-done | bytes 32800 | tf_op jit(solution)/shard_map/ppermute | solution.py:339
  55.5 0.8 %collective-permute-done.7 = bf16[16,1024]{1,0:T(8,128)(2,1)S(1)} collective-permute-done((bf16[16,1024]{1,0:T(8,128)(2,1)S(1)}, bf16[16,1024]{1,0:T(8,128)(2,1)S(1)}, u32[]{:S(2)}, u32[]{:S(2)}) %collective-permute-start.7) | collective-permute-done | bytes 32800 | tf_op jit(solution)/shard_map/ppermute | solution.py:339
  56.4 7.8 %weight_grads.1 = (bf16[2,1024,2048]{2,1,0:T(8,128)(2,1)}, bf16[2,2048,1024]{2,1,0:T(8,128)(2,1)}) custom-call(bf16[4,32,1024]{2,1,0:T(8,128)(2,1)S(1)} %bitcast.12, bf16[4,32,1024]{2,1,0:T(8,128)(2,1)S(1)} %bitcast.13, bf16[2,32,2048]{2,1,0:T(8,128)(2,1)S(1)} %get-tuple-element.28.hid_ref, bf16[2,32,2048]{2,1,0:T(8,128)(2,1)S(1)} %get-tuple-element.29.dpre_ref), custom_call_target="tpu_custom_call" | custom-call | tf_op jit(solution)/shard_map/weight_grads/pallas_call | solution.py:315
  64.3 1.3 %token_grads.1 = bf16[1,256,1024]{2,1,0:T(8,128)(2,1)} custom-call(f32[1,64,256]{2,1,0:T(8,128)S(1)} %get-tuple-element.18.refs_2_.refs_0_, bf16[1,64,1024]{2,1,0:T(8,128)(2,1)S(1)} %get-tuple-element.24.refs_1_, bf16[1,32,256]{2,1,0:T(8,128)(2,1)S(1)} %get-tuple-element.25.refs_2_, bf16[32,1024]{1,0:T(8,128)(2,1)S(1)} %bitcast.16), custom_call_target="tpu_custom_call" | custom-call | tf_op jit(solution)/shard_map/token_grads/pallas_call | solution.py:186
  65.6 0.7 %maximum_bitcast_fusion = f32[1024,32]{0,1:T(8,128)} fusion(f32[16,1024]{1,0:T(8,128)S(1)} %get-tuple-element.33, f32[16,1024]{1,0:T(8,128)S(1)} %get-tuple-element.32), kind=kLoop, calls=%fused_computation.1 | loop fusion | flops 32768 | bytes 262144 | tf_op jit(solution)/shard_map/transpose | solution.py:439
  (18 shorter events, 0.6 us)
Async XLA Ops:
  18.9 1.3 %collective-permute-start = (bf16[16,4,1024]{2,1,0:T(4,128)(2,1)S(1)}, bf16[16,4,1024]{2,1,0:T(4,128)(2,1)S(1)}, u32[]{:S(2)}, u32[]{:S(2)}) collective-permute-start(bf16[16,4,1024]{2,1,0:T(4,128)(2,1)S(1)} %all_to_all.10), channel_id=1, source_target_pairs={{0,16},{16,0},{1,17},{17,1},{2,18},{18,2},{3,19},{19,3},{4,20},{20... | collective-permute-start | bytes 393224 | tf_op jit(solution)/shard_map/ppermute | solution.py:339
  20.5 20.5 %copy-start = (bf16[1,256,1024]{2,1,0:T(8,128)(2,1)S(1)}, bf16[1,256,1024]{2,1,0:T(8,128)(2,1)}, u32[]{:S(2)}) copy-start(bf16[1,256,1024]{2,1,0:T(8,128)(2,1)} %refs_3_.5) | copy-start | bytes 1572868
  20.5 20.5 %copy-start.1 = (bf16[1,256,1024]{2,1,0:T(8,128)(2,1)S(1)}, bf16[1,256,1024]{2,1,0:T(8,128)(2,1)}, u32[]{:S(2)}) copy-start(bf16[1,256,1024]{2,1,0:T(8,128)(2,1)} %refs_4_.5) | copy-start | bytes 1572868
  20.5 43.8 %copy-start.2 = (bf16[1024,32]{0,1:T(8,128)(2,1)S(1)}, bf16[1024,32]{0,1:T(8,128)(2,1)}, u32[]{:S(2)}) copy-start(bf16[1024,32]{0,1:T(8,128)(2,1)} %param.6) | copy-start | bytes 196612
  27.2 1.4 %collective-permute-start.1 = (bf16[4,16,1024]{2,1,0:T(8,128)(2,1)S(1)}, bf16[4,16,1024]{2,1,0:T(8,128)(2,1)S(1)}, u32[]{:S(2)}, u32[]{:S(2)}) collective-permute-start(bf16[4,16,1024]{2,1,0:T(8,128)(2,1)S(1)} %get-tuple-element.23), channel_id=1, source_target_pairs={{0,16},{16,0},{1,17},{17,1},{2,18},{18,2},{3,19},{19,3},{4,20},{20... | collective-permute-start | bytes 393224 | tf_op jit(solution)/shard_map/ppermute | solution.py:339
  29.5 11.5 %all-to-all-start.1 = ((bf16[16,4,1024]{2,1,0:T(4,128)(2,1)}), bf16[16,4,1024]{2,1,0:T(4,128)(2,1)S(1)}, u32[]{:S(2)}, u32[]{:S(2)}) async-start(bf16[16,4,1024]{2,1,0:T(4,128)(2,1)} %join.1), calls=%async_computation.1 | async-start | bytes 262144 | tf_op jit(solution)/shard_map/all_to_all | solution.py:433
  41.8 1.3 %collective-permute-start.2 = (bf16[16,1024]{1,0:T(8,128)(2,1)S(1)}, bf16[16,1024]{1,0:T(8,128)(2,1)S(1)}, u32[]{:S(2)}, u32[]{:S(2)}) collective-permute-start(bf16[16,1024]{1,0:T(8,128)(2,1)S(1)} %get-tuple-element.27), channel_id=1, source_target_pairs={{0,16},{16,0},{1,17},{17,1},{2,18},{18,2},{3,19},{19,3},{4,20},{20... | collective-permute-start | bytes 98312 | tf_op jit(solution)/shard_map/ppermute | solution.py:339
  43.1 5.2 %collective-permute-start.5 = (bf16[16,1024]{1,0:T(8,128)(2,1)S(1)}, bf16[16,1024]{1,0:T(8,128)(2,1)S(1)}, u32[]{:S(2)}, u32[]{:S(2)}) collective-permute-start(bf16[16,1024]{1,0:T(8,128)(2,1)S(1)} %add_convert_fusion.2), channel_id=1, source_target_pairs={{0,3},{1,2},{2,1},{3,0},{4,7},{5,6},{6,5},{7,4},{8,11},{9,10},{10,... | collective-permute-start | bytes 98312 | tf_op jit(solution)/shard_map/ppermute | solution.py:339
  43.9 4.4 %collective-permute-start.4 = (bf16[16,1024]{1,0:T(8,128)(2,1)S(1)}, bf16[16,1024]{1,0:T(8,128)(2,1)S(1)}, u32[]{:S(2)}, u32[]{:S(2)}) collective-permute-start(bf16[16,1024]{1,0:T(8,128)(2,1)S(1)} %add_convert_fusion.2), channel_id=1, source_target_pairs={{0,2},{1,3},{2,0},{3,1},{4,6},{5,7},{6,4},{7,5},{8,10},{9,11},{10,... | collective-permute-start | bytes 98312 | tf_op jit(solution)/shard_map/ppermute | solution.py:339
  45.7 3.9 %collective-permute-start.3 = (bf16[16,1024]{1,0:T(8,128)(2,1)S(1)}, bf16[16,1024]{1,0:T(8,128)(2,1)S(1)}, u32[]{:S(2)}, u32[]{:S(2)}) collective-permute-start(bf16[16,1024]{1,0:T(8,128)(2,1)S(1)} %add_convert_fusion.2), channel_id=1, source_target_pairs={{0,1},{1,0},{2,3},{3,2},{4,5},{5,4},{6,7},{7,6},{8,9},{9,8},{10,11... | collective-permute-start | bytes 98312 | tf_op jit(solution)/shard_map/ppermute | solution.py:339
  49.7 5.8 %collective-permute-start.8 = (bf16[16,1024]{1,0:T(8,128)(2,1)S(1)}, bf16[16,1024]{1,0:T(8,128)(2,1)S(1)}, u32[]{:S(2)}, u32[]{:S(2)}) collective-permute-start(bf16[16,1024]{1,0:T(8,128)(2,1)S(1)} %add_convert_fusion.1), channel_id=1, source_target_pairs={{0,12},{1,13},{2,14},{3,15},{4,8},{5,9},{6,10},{7,11},{8,4},{9,5},... | collective-permute-start | bytes 98312 | tf_op jit(solution)/shard_map/ppermute | solution.py:339
  50.8 5.5 %collective-permute-start.7 = (bf16[16,1024]{1,0:T(8,128)(2,1)S(1)}, bf16[16,1024]{1,0:T(8,128)(2,1)S(1)}, u32[]{:S(2)}, u32[]{:S(2)}) collective-permute-start(bf16[16,1024]{1,0:T(8,128)(2,1)S(1)} %add_convert_fusion.1), channel_id=1, source_target_pairs={{0,8},{1,9},{2,10},{3,11},{4,12},{5,13},{6,14},{7,15},{8,0},{9,1},... | collective-permute-start | bytes 98312 | tf_op jit(solution)/shard_map/ppermute | solution.py:339
  51.4 4.9 %collective-permute-start.6 = (bf16[16,1024]{1,0:T(8,128)(2,1)S(1)}, bf16[16,1024]{1,0:T(8,128)(2,1)S(1)}, u32[]{:S(2)}, u32[]{:S(2)}) collective-permute-start(bf16[16,1024]{1,0:T(8,128)(2,1)S(1)} %add_convert_fusion.1), channel_id=1, source_target_pairs={{0,4},{1,5},{2,6},{3,7},{4,0},{5,1},{6,2},{7,3},{8,12},{9,13},{10,... | collective-permute-start | bytes 98312 | tf_op jit(solution)/shard_map/ppermute | solution.py:339
  56.4 9.2 %collective-permute-start.9 = (bf16[16,1024]{1,0:T(8,128)(2,1)S(1)}, bf16[16,1024]{1,0:T(8,128)(2,1)S(1)}, u32[]{:S(2)}, u32[]{:S(2)}) collective-permute-start(bf16[16,1024]{1,0:T(8,128)(2,1)S(1)} %add_convert_fusion), channel_id=1, source_target_pairs={{0,16},{16,0},{1,17},{17,1},{2,18},{18,2},{3,19},{19,3},{4,20},{20... | collective-permute-start | bytes 98312 | tf_op jit(solution)/shard_map/ppermute | solution.py:339

commit v3 on v2

v3 whole, which is shorter than its diff:
```python
import jax
import jax.numpy as jnp
from jax import lax
from jax.experimental import pallas as pl
from jax.experimental.pallas import tpu as pltpu
from jax.sharding import PartitionSpec as P


def gelu_parts(pre):
    cdf = 0.5 * (1.0 + lax.erf(pre * 0.7071067811865476))
    slope = cdf + pre * jnp.exp(-0.5 * pre * pre) * 0.3989422804014327
    return (pre * cdf, slope)


def softmax_along(values, axis):
    top = jnp.max(values, axis=axis, keepdims=True)
    expo = jnp.exp(values - top)
    return expo / jnp.sum(expo, axis=axis, keepdims=True)


def dot(a, b, contract):
    return lax.dot_general(a, b, (contract, ((), ())), preferred_element_type=jnp.float32)


def in_hbm(value):
    return pltpu.with_memory_space_constraint(value, pltpu.HBM)


NN, NT, TN = ((1,), (0,)), ((1,), (1,)), ((0,), (0,))


def chunk_count(size, wanted):
    while size % wanted or (size // wanted) % 256 and wanted > 1:
        wanted -= 1
    return wanted


CHUNKS, AHEAD, FLIGHT = 8, 2, 8


def first_columns(hid):
    chunks = chunk_count(hid, CHUNKS)
    return min(AHEAD, chunks) * (hid // chunks)


def route_kernel(
    mine, tok_hbm, out_hbm, par_hbm, sent_ref, disp_ref, comb_ref, tok_v, out_v, par_v, sems
):
    slots = par_v.shape[0]
    loads = [
        pltpu.make_async_copy(par_hbm, par_v, sems.at[0]),
        pltpu.make_async_copy(tok_hbm, tok_v, sems.at[1]),
        pltpu.make_async_copy(out_hbm, out_v, sems.at[2]),
    ]
    for load in loads:
        load.start()
    loads[0].wait()
    loads[1].wait()
    for image in range(tok_v.shape[0]):
        tok = tok_v[image]
        logits = dot(par_v[...], tok, NT)
        dispatch = softmax_along(logits, 1)
        combine = softmax_along(logits, 0)
        disp_ref[image] = dispatch
        comb_ref[image] = combine
        slot_in = dot(dispatch.astype(jnp.bfloat16), tok, NN)
        if image == 0:
            loads[2].wait()
        slot_cot = dot(combine.astype(jnp.bfloat16), out_v[image], NN)
        for kind, values in enumerate((slot_in, slot_cot)):
            for k in range(slots // mine):
                sent_ref[kind * (slots // mine) + k, image] = values[mine * k : mine * (k + 1)].astype(jnp.bfloat16)


def route_forward(tokens, grad_out, param_t, owners):
    images, patches, width = tokens.shape
    slots = param_t.shape[0]
    mine = slots // owners
    vmem = pl.BlockSpec(memory_space=pltpu.VMEM)
    hbm = pl.BlockSpec(memory_space=pl.ANY)
    return pl.pallas_call(
        lambda *refs: route_kernel(mine, *refs),
        in_specs=[hbm] * 3,
        out_specs=[vmem] * 3,
        out_shape=[
            jax.ShapeDtypeStruct((2 * owners, images, mine, width), jnp.bfloat16),
            jax.ShapeDtypeStruct((images, slots, patches), jnp.float32),
            jax.ShapeDtypeStruct((images, slots, patches), jnp.float32),
        ],
        scratch_shapes=[
            pltpu.VMEM(tokens.shape, jnp.bfloat16),
            pltpu.VMEM(grad_out.shape, jnp.bfloat16),
            pltpu.VMEM(param_t.shape, jnp.bfloat16),
            pltpu.SemaphoreType.DMA((3,)),
        ],
        compiler_params=pltpu.CompilerParams(vmem_limit_bytes=16 << 20),
        name="route_forward",
    )(in_hbm(tokens), in_hbm(grad_out), in_hbm(param_t))


def fetch_kernel(win_hbm, wout_hbm, win_v, wout_v, sems):
    first = win_v.shape[1]
    loads = (
        pltpu.make_async_copy(win_hbm.at[0, :, pl.ds(0, first)], win_v, sems.at[0]),
        pltpu.make_async_copy(wout_hbm.at[0, pl.ds(0, first), :], wout_v, sems.at[1]),
    )
    for load in loads:
        load.start()
    for load in loads:
        load.wait()


def fetch_first(weight_in, weight_out):
    width = weight_in.shape[1]
    first = first_columns(weight_in.shape[2])
    return pl.pallas_call(
        fetch_kernel,
        in_specs=[pl.BlockSpec(memory_space=pl.ANY)] * 2,
        out_specs=[pl.BlockSpec(memory_space=pltpu.VMEM)] * 2,
        out_shape=[
            jax.ShapeDtypeStruct((width, first), jnp.bfloat16),
            jax.ShapeDtypeStruct((first, width), jnp.bfloat16),
        ],
        scratch_shapes=[pltpu.SemaphoreType.DMA((2,))],
        compiler_params=pltpu.CompilerParams(vmem_limit_bytes=8 << 20),
        name="fetch_first",
    )(in_hbm(weight_in), in_hbm(weight_out))


def route_back_kernel(
    side_ref, back_ref, disp_ref, comb_ref, tok_ref, out_ref, grad_ref, dl_ref, keep_ref, give_ref, raw, part
):
    blocks, _, mine, _ = back_ref.shape
    slots = blocks // 2 * mine
    total = None
    for image in range(tok_ref.shape[0]):
        for k in range(blocks):
            raw[mine * k : mine * (k + 1), :] = back_ref[k, image].astype(jnp.float32)
        grad_slot = raw[:slots, :].astype(jnp.bfloat16)
        slot_out = raw[slots:, :].astype(jnp.bfloat16)
        grad_ref[image] = grad_slot
        tok = tok_ref[image]
        dispatch = disp_ref[image]
        combine = comb_ref[image]
        d_dispatch = dot(grad_slot, tok, NT)
        d_combine = dot(slot_out, out_ref[image], NT)
        d_logits = dispatch * (d_dispatch - jnp.sum(dispatch * d_dispatch, axis=1, keepdims=True))
        d_logits = d_logits + combine * (d_combine - jnp.sum(combine * d_combine, axis=0, keepdims=True))
        dl = d_logits.astype(jnp.bfloat16)
        dl_ref[image] = dl
        local = dot(dl, tok, NN)
        total = local if total is None else total + local
    half = slots // 2
    part[...] = total
    side = side_ref[0]
    keep_ref[...] = part[pl.ds(pl.multiple_of(side * half, half), half), :].astype(jnp.bfloat16)
    give_ref[...] = part[pl.ds(pl.multiple_of((1 - side) * half, half), half), :].astype(jnp.bfloat16)


def route_back(side, back, dispatch, combine, tokens, grad_out):
    blocks, images, mine, width = back.shape
    slots = blocks // 2 * mine
    vmem = pl.BlockSpec(memory_space=pltpu.VMEM)
    return pl.pallas_call(
        route_back_kernel,
        in_specs=[pl.BlockSpec(memory_space=pltpu.SMEM)] + [vmem] * 5,
        out_specs=[vmem] * 4,
        out_shape=[
            jax.ShapeDtypeStruct((images, slots, width), jnp.bfloat16),
            jax.ShapeDtypeStruct((images, slots, tokens.shape[1]), jnp.bfloat16),
            jax.ShapeDtypeStruct((slots // 2, width), jnp.bfloat16),
            jax.ShapeDtypeStruct((slots // 2, width), jnp.bfloat16),
        ],
        scratch_shapes=[
            pltpu.VMEM((2 * slots, width), jnp.float32),
            pltpu.VMEM((slots, width), jnp.float32),
        ],
        compiler_params=pltpu.CompilerParams(vmem_limit_bytes=16 << 20),
        name="route_back",
    )(side, back, dispatch, combine, tokens, grad_out)


def token_grad_kernel(disp_ref, slot_ref, dl_ref, par_ref, grad_ref):
    left = jnp.concatenate((disp_ref[0].astype(jnp.bfloat16), dl_ref[0]), axis=0)
    right = jnp.concatenate((slot_ref[0], par_ref[...]), axis=0)
    grad_ref[0] = dot(left, right, TN).astype(jnp.bfloat16)


def token_grads(dispatch, grad_slot, dl, param_t):
    images, slots, patches = dispatch.shape
    width = param_t.shape[1]
    table = pl.BlockSpec((1, slots, patches), lambda i: (i, 0, 0))
    return pl.pallas_call(
        token_grad_kernel,
        grid=(images,),
        in_specs=[
            table,
            pl.BlockSpec((1, slots, width), lambda i: (i, 0, 0)),
            table,
            pl.BlockSpec((slots, width), lambda i: (0, 0)),
        ],
        out_specs=pl.BlockSpec((1, patches, width), lambda i: (i, 0, 0)),
        out_shape=jax.ShapeDtypeStruct((images, patches, width), jnp.bfloat16),
        compiler_params=pltpu.CompilerParams(vmem_limit_bytes=16 << 20),
        name="token_grads",
    )(dispatch, grad_slot, dl, param_t)


def expert_body(
    experts, chunks, place_ref, x_ref, first_in, first_out, win_hbm, wout_hbm,
    keep_ref, give_ref, hid_ref, dpre_ref, win_v, wout_v, win_t, wout_t, sems,
):
    place = place_ref[0]
    step = win_v.shape[2] // chunks
    order = [(e, c) for e in range(experts) for c in range(chunks)]
    held = first_in.shape[1] // step

    def copies(k):
        e, c = order[k]
        cols = pl.ds(c * step, step)
        return (
            pltpu.make_async_copy(win_hbm.at[e, :, cols], win_v.at[e, :, cols], sems.at[0, e, c]),
            pltpu.make_async_copy(wout_hbm.at[e, cols, :], wout_v.at[e, cols, :], sems.at[1, e, c]),
        )

    def start(k):
        if k < len(order):
            for copy in copies(k):
                copy.start()

    def weights(k):
        e, c = order[k]
        cols = pl.ds(c * step, step)
        if k < held:
            return first_in.at[:, cols], first_out.at[cols, :]
        return win_v.at[e, :, cols], wout_v.at[e, cols, :]

    groups = {held: 1}
    k = held + 1
    while k < len(order):
        groups[k] = min(2, len(order) - k)
        k += groups[k]

    for k in range(held, held + FLIGHT):
        start(k)
    ready = out = grad = None
    for k in range(len(order) + 1):
        for arriving in range(k, k + groups.get(k, 0)):
            if arriving < len(order):
                for copy in copies(arriving):
                    copy.wait()
                start(arriving + FLIGHT)
        before = ready
        if k < len(order):
            w1, w2 = weights(k)
            e = order[k][0]
            win_t[k] = w1[...].T
            wout_t[k] = w2[...].T
            x = x_ref[place * experts + e]
            g = x_ref[(1 - place) * experts + e]
            ready = dot(x, w1[...], NN), dot(g, wout_t[k], NN)
        if before is None:
            continue
        e, c = order[k - 1]
        w2 = weights(k - 1)[1]
        cols = pl.ds(c * step, step)
        pre, back = before
        value, slope = gelu_parts(pre)
        hidden = value.astype(jnp.bfloat16)
        dpre = (back * slope).astype(jnp.bfloat16)
        hid_ref[e, :, cols] = hidden
        dpre_ref[e, :, cols] = dpre
        o = dot(hidden, w2[...], NN)
        d = dot(dpre, win_t[k - 1], NN)
        out, grad = (o, d) if c == 0 else (out + o, grad + d)
        if c == chunks - 1:
            if keep_ref.shape[0] == experts:
                first = place == 0
                keep_ref[e] = jnp.where(first, grad, out)
                give_ref[e] = jnp.where(first, out, grad).astype(jnp.bfloat16)
            else:
                keep_ref[e] = grad
                keep_ref[experts + e] = out
                give_ref[e] = grad.astype(jnp.bfloat16)


def expert_forward(place, rows_in, first_in, first_out, weight_in, weight_out, split):
    experts, width, hid = weight_in.shape
    rows = rows_in.shape[1]
    chunks = chunk_count(hid, CHUNKS)
    vmem = pl.BlockSpec(memory_space=pltpu.VMEM)
    hbm = pl.BlockSpec(memory_space=pl.ANY)
    return pl.pallas_call(
        lambda *refs: expert_body(experts, chunks, *refs),
        in_specs=[pl.BlockSpec(memory_space=pltpu.SMEM), vmem, vmem, vmem, hbm, hbm],
        out_specs=[vmem, vmem, vmem, vmem],
        out_shape=[
            jax.ShapeDtypeStruct((experts if split else 2 * experts, rows, width), jnp.float32),
            jax.ShapeDtypeStruct((experts, rows, width), jnp.bfloat16),
            jax.ShapeDtypeStruct((experts, rows, hid), jnp.bfloat16),
            jax.ShapeDtypeStruct((experts, rows, hid), jnp.bfloat16),
        ],
        scratch_shapes=[
            pltpu.VMEM((experts, width, hid), jnp.bfloat16),
            pltpu.VMEM((experts, hid, width), jnp.bfloat16),
            pltpu.VMEM((experts * chunks, hid // chunks, width), jnp.bfloat16),
            pltpu.VMEM((experts * chunks, width, hid // chunks), jnp.bfloat16),
            pltpu.SemaphoreType.DMA((2, experts, chunks)),
        ],
        compiler_params=pltpu.CompilerParams(vmem_limit_bytes=40 << 20),
        name="expert_forward",
    )(place, rows_in, first_in, first_out, in_hbm(weight_in), in_hbm(weight_out))


def weight_grad_kernel(experts, place_ref, rows_ref, hid_ref, dpre_ref, gin_ref, gout_ref):
    e = pl.program_id(0)
    x = rows_ref[place_ref[0] * experts + e]
    g = rows_ref[(1 - place_ref[0]) * experts + e]
    gin_ref[0] = dot(x, dpre_ref[0], TN).astype(jnp.bfloat16)
    gout_ref[0] = dot(hid_ref[0], g, TN).astype(jnp.bfloat16)


def weight_grads(place, rows_in, hidden, dpre):
    experts, rows, hid = hidden.shape
    width = rows_in.shape[2]
    chunks = chunk_count(hid, 4)
    step = hid // chunks
    return pl.pallas_call(
        lambda *refs: weight_grad_kernel(experts, *refs),
        grid=(experts, chunks),
        in_specs=[
            pl.BlockSpec(memory_space=pltpu.SMEM),
            pl.BlockSpec((2 * experts, rows, width), lambda e, c: (0, 0, 0)),
            pl.BlockSpec((1, rows, step), lambda e, c: (e, 0, c)),
            pl.BlockSpec((1, rows, step), lambda e, c: (e, 0, c)),
        ],
        out_specs=[
            pl.BlockSpec((1, width, step), lambda e, c: (e, 0, c)),
            pl.BlockSpec((1, step, width), lambda e, c: (e, c, 0)),
        ],
        out_shape=[
            jax.ShapeDtypeStruct((experts, width, hid), jnp.bfloat16),
            jax.ShapeDtypeStruct((experts, hid, width), jnp.bfloat16),
        ],
        compiler_params=pltpu.CompilerParams(vmem_limit_bytes=24 << 20),
        name="weight_grads",
    )(place, rows_in, hidden, dpre)


def swap(value, axis, mask):
    size = lax.axis_size(axis)
    return lax.ppermute(value, axis, [(k, k ^ mask) for k in range(size)])


def is_pow2(n):
    return n & (n - 1) == 0


def sum_bits(acc, axis, first_bit):
    size = lax.axis_size(axis)
    bit = first_bit
    while bit < size:
        sent = acc.astype(jnp.bfloat16)
        own = sent.astype(jnp.float32)
        if 2 * bit < size:
            got = []
            for mask in (bit, 2 * bit, 3 * bit):
                got.append(swap(sent, axis, mask).astype(jnp.float32))
            a, b, c = got
            acc = (own + a) + (b + c)
            bit *= 4
        else:
            acc = own + swap(sent, axis, bit).astype(jnp.float32)
            bit *= 2
    return acc


def sum_everywhere(keep, give, side):
    ex, ey = lax.axis_size("ex"), lax.axis_size("ey")
    if not (is_pow2(ex) and is_pow2(ey)):
        low = jnp.where(side == 0, keep, give).astype(jnp.float32)
        high = jnp.where(side == 0, give, keep).astype(jnp.float32)
        return lax.psum(jnp.concatenate((low, high), axis=0), ("ex", "ey"))
    acc = keep.astype(jnp.float32) + swap(give, "ex", 1).astype(jnp.float32)
    acc = sum_bits(acc, "ex", 2)
    acc = sum_bits(acc, "ey", 1)
    sent = acc.astype(jnp.bfloat16)
    own = sent.astype(jnp.float32)
    other = swap(sent, "ex", 1)
    other = other.astype(jnp.float32)
    return jnp.concatenate((jnp.where(side == 0, own, other), jnp.where(side == 0, other, own)), axis=0)


def join_kernel(keep_ref, got_ref, sum_hbm, sum_v, sem):
    block, rows, width = keep_ref.shape
    total = (keep_ref[...] + got_ref[...].astype(jnp.float32)).reshape(block * rows, width)
    shape = (block * rows, block * rows)
    to = lax.broadcasted_iota(jnp.int32, shape, 0)
    at = lax.broadcasted_iota(jnp.int32, shape, 1)
    move = jnp.where((to % block) * rows + to // block == at, 1.0, 0.0).astype(jnp.bfloat16)
    moved = dot(move, total.astype(jnp.bfloat16), NN)
    for k in range(rows):
        sum_v[k] = moved[block * k : block * (k + 1)].astype(jnp.bfloat16)
    copy = pltpu.make_async_copy(sum_v, sum_hbm, sem)
    copy.start()
    copy.wait()


def join(keep, got):
    block, rows, width = keep.shape
    vmem = pl.BlockSpec(memory_space=pltpu.VMEM)
    return pl.pallas_call(
        join_kernel,
        in_specs=[vmem, vmem],
        out_specs=pl.BlockSpec(memory_space=pl.ANY),
        out_shape=pltpu.HBM((rows, block, width), jnp.bfloat16),
        scratch_shapes=[pltpu.VMEM((rows, block, width), jnp.bfloat16), pltpu.SemaphoreType.DMA],
        compiler_params=pltpu.CompilerParams(vmem_limit_bytes=16 << 20),
        name="join",
    )(keep, got)


def per_device(tokens, slot_param, weight_in, weight_out, grad_out):
    ex, ey = lax.axis_size("ex"), lax.axis_size("ey")
    images, _, width = tokens.shape
    slots = slot_param.shape[1]
    mine = slots // ey
    param_t = slot_param.T
    sent, dispatch, combine = route_forward(tokens, grad_out, param_t, ey)
    first_in, first_out = fetch_first(weight_in, weight_out)
    side = lax.axis_index("ex") % 2
    rows = ex * ey * images
    paired = ex == 2
    if paired:
        sent = sent.reshape(2 * ey, images * mine, width)
        own = lax.all_to_all(sent, ("ex", "ey"), split_axis=0, concat_axis=0, tiled=True)
        other = swap(own, "ex", 1)
        place = side.reshape(1)
        kinds = jnp.stack((own, other))
        rows_in = kinds.reshape(2, rows, mine, width).transpose(0, 2, 1, 3).reshape(2 * mine, rows, width)
    else:
        place = jnp.zeros((1,), jnp.int32)
        sent = sent.reshape(2, ey, images, mine, width).transpose(1, 2, 0, 3, 4)
        sent = sent.reshape(ey * images, 2 * mine, width)
        moved = lax.all_to_all(sent, "ey", split_axis=0, concat_axis=0, tiled=True)
        arrived = lax.all_gather(moved, "ex", axis=0)
        rows_in = arrived.reshape(rows, 2 * mine, width).transpose(1, 0, 2)
    keep_rows, give_rows, hidden, dpre = expert_forward(
        place, rows_in, first_in, first_out, weight_in, weight_out, paired
    )
    if paired:
        summed = join(keep_rows, swap(give_rows, "ex", 1)).reshape(2 * ey, images * mine, width)
        back = lax.all_to_all(summed, ("ex", "ey"), split_axis=0, concat_axis=0, tiled=True)
        back = back.reshape(2 * ey, images, mine, width)
    else:
        blocks = keep_rows.astype(jnp.bfloat16).transpose(1, 0, 2).reshape(ex, ey * images, 2 * mine, width)
        summed = lax.psum_scatter(blocks, "ex", scatter_dimension=0)
        back = lax.all_to_all(summed, "ey", split_axis=0, concat_axis=0, tiled=True)
        back = back.reshape(ey, images, 2, mine, width).transpose(2, 0, 1, 3, 4)
        back = back.reshape(2 * ey, images, mine, width)
    grad_win, grad_wout = weight_grads(place, rows_in, hidden, dpre)
    grad_slot, logit_grad, keep, give = route_back(side.reshape(1), back, dispatch, combine, tokens, grad_out)
    grad_param = sum_everywhere(keep, give, side).T
    grad_tokens = token_grads(dispatch, grad_slot, logit_grad, param_t)
    return (grad_tokens, grad_param, grad_win, grad_wout)


def solution(mesh):
    in_specs = (
        P(("ex", "ey"), None, None),
        P(),
        P("ey", None, "ex"),
        P("ey", "ex", None),
        P(("ex", "ey"), None, None),
    )
    out_specs = (P(("ex", "ey"), None, None), P(), P("ey", None, "ex"), P("ey", "ex", None))

    return jax.shard_map(per_device, mesh=mesh, in_specs=in_specs, out_specs=out_specs, check_vma=False)
```

time: 66.5 us -> 65.8 us (0.989)
  blocking collectives: 15.9 us -> 25.7 us
  waiting for transfers between devices: 16.9 us -> 8.17 us
  starting transfers between devices: 11.9 us -> 8.72 us
  Pallas kernels: 19.7 us -> 21 us
    all_to_all x1 -> x2, blocking collectives: 15.9 us -> 25.7 us  [the longest x1 15.1 us: per_device(): lax.all_to_all(sent, ('ex', 'ey'), split_axis=0, concat_axis=0, tiled=True)]
    all_to_all x1 -> x0, waiting for transfers between devices: 7.99 us -> none  [per_device(): back = lax.all_to_all(summed, 'ey', split_axis=0, concat_axis=0, tiled=True)]
    all_to_all x1 -> x0, starting transfers between devices: 3.52 us -> none  [per_device(): back = lax.all_to_all(summed, 'ey', split_axis=0, concat_axis=0, tiled=True)]
    pallas_call x4 -> x5, Pallas kernels: 10.8 us -> 12.1 us  [the longest x1 7.85 us: weight_grads(): pl.pallas_call(lambda *refs: weight_grad_kernel(experts, *refs), grid=(ex...]
    ppermute x10, waiting for transfers between devices: 8.92 us -> 8.17 us  [swap(): return lax.ppermute(value, axis, [(k, k ^ mask) for k in range(size)])]
  transfers between devices with their start and end apart: 11 -> 10, of which waited for: 9 -> 7; matrix products, arithmetic and copies ran while one was open for 0% -> 0% of each run, Pallas kernels for 14% -> 16%
where the time goes in v3:
time: 65.8 us; the launch traced here: 65.5 us
  blocking collectives  25.7 us (39%)
  Pallas kernels  21 us (32%)
  starting transfers between devices  8.72 us (13%)
  waiting for transfers between devices  8.17 us (12%)
  other arithmetic  1.1 us (2%)
  between operations  0.76 us (1%)
    all_to_all x1, blocking collectives, per_device(): lax.all_to_all(sent, ('ex', 'ey'), split_axis=0, concat_axis=0, tiled=True)  15.1 us
    all_to_all x1, blocking collectives, per_device(): lax.all_to_all(summed, ('ex', 'ey'), split_axis=0, concat_axis=0, tiled=T...  10.6 us
    ppermute x10, starting transfers between devices, swap(): return lax.ppermute(value, axis, [(k, k ^ mask) for k in range(size)])  8.72 us
    ppermute x10, waiting for transfers between devices, swap(): return lax.ppermute(value, axis, [(k, k ^ mask) for k in range(size)])  8.17 us
    pallas_call x1, Pallas kernels, weight_grads(): pl.pallas_call(lambda *refs: weight_grad_kernel(experts, *refs), grid=(ex...  7.85 us
    pallas_call x1, Pallas kernels, expert_forward(): pl.pallas_call(lambda *refs: expert_body(experts, chunks, *refs), in_spec...  6.81 us
    pallas_call x1, Pallas kernels, route_forward(): pl.pallas_call(lambda *refs: route_kernel(mine, *refs), in_specs=[hbm] *...  2.16 us
    pallas_call x1, Pallas kernels, fetch_first(): pl.pallas_call(fetch_kernel, in_specs=[pl.BlockSpec(memory_space=pl.ANY)]...  1.57 us
  transfers between devices with their start and end apart: 10, of which 7 were waited for; matrix products, arithmetic and copies ran while one was open for 0% of the time, Pallas kernels for 16%

profile of v3, /device:TPU:0, one launch (start us, length us, event | category | flops | bytes accessed | tf_op | source)
XLA Modules:
  0.0 65.5 jit_solution(17718328245827431597)
XLA Ops:
  0.6 2.2 %route_forward.1 = (bf16[32,1,2,1024]{3,2,1,0:T(2,128)(2,1)S(1)}, f32[1,32,256]{2,1,0:T(8,128)S(1)}, f32[1,32,256]{2,1,0:T(8,128)S(1)}) custom-call(bf16[1,256,1024]{2,1,0:T(8,128)(2,1)} %tok_ref.1, bf16[1,256,1024]{2,1,0:T(8,128)(2,1)} %out_ref.1, bf16[32,1024]{1,0:T(8,128)(2,1)} %bitcast.14), custom_call_target="tpu_custom_call" | custom-call | tf_op jit(solution)/shard_map/route_forward/pallas_call | solution.py:81
  2.8 15.1 %all_to_all.10 = bf16[32,2,1024]{2,1,0:T(2,128)(2,1)S(1)} all-to-all(bf16[32,2,1024]{2,1,0:T(2,128)(2,1)S(1)} %bitcast.16), channel_id=1, replica_groups=mesh['ex'=2,'ey'=16] {'ex','ey'}, dimensions={0} | all-to-all | bytes 262144 | tf_op jit(solution)/shard_map/all_to_all | solution.py:436
  17.9 1.6 %fetch_first.1 = (bf16[1024,512]{1,0:T(8,128)(2,1)S(1)}, bf16[512,1024]{1,0:T(8,128)(2,1)S(1)}) custom-call(bf16[2,1024,2048]{2,1,0:T(8,128)(2,1)} %refs_4_.1, bf16[2,2048,1024]{2,1,0:T(8,128)(2,1)} %refs_5_.1), custom_call_target="tpu_custom_call" | custom-call | tf_op jit(solution)/shard_map/fetch_first/pallas_call | solution.py:116
  20.0 6.8 %expert_forward.1 = (f32[2,32,1024]{2,1,0:T(8,128)S(1)}, bf16[2,32,1024]{2,1,0:T(8,128)(2,1)S(1)}, bf16[2,32,2048]{2,1,0:T(8,128)(2,1)S(1)}, bf16[2,32,2048]{2,1,0:T(8,128)(2,1)S(1)}) custom-call(s32[1]{0:T(128)} %bitcast.1.refs_0_.side_ref, bf16[4,32,1024]{2,1,0:T(8,128)(2,1)S(1)} %bitcast.11, bf16[1024,512]{1,0:T(8,128)(2,1)S(1)} %get-tuple-element.21.refs_2_, ...), custom_call_target="tpu_custom_call" | custom-call | tf_op jit(solution)/shard_map/expert_forward/pallas_call | solution.py:293
  26.8 0.6 collective-permute-start.1
  27.4 1.0 %collective-permute-done.1.got_ref = bf16[2,32,1024]{2,1,0:T(8,128)(2,1)S(1)} collective-permute-done((bf16[2,32,1024]{2,1,0:T(8,128)(2,1)S(1)}, bf16[2,32,1024]{2,1,0:T(8,128)(2,1)S(1)}, u32[]{:S(2)}, u32[]{:S(2)}) %collective-permute-start.1) | collective-permute-done | bytes 131104 | tf_op jit(solution)/shard_map/ppermute | solution.py:352
  28.3 0.8 %join.1 = bf16[32,2,1024]{2,1,0:T(2,128)(2,1)} custom-call(f32[2,32,1024]{2,1,0:T(8,128)S(1)} %get-tuple-element.23.keep_ref, bf16[2,32,1024]{2,1,0:T(8,128)(2,1)S(1)} %collective-permute-done.1.got_ref), custom_call_target="tpu_custom_call" | custom-call | tf_op jit(solution)/shard_map/join/pallas_call | solution.py:412
  29.2 10.6 %all_to_all.11 = bf16[32,2,1024]{2,1,0:T(2,128)(2,1)S(1)} all-to-all(bf16[32,2,1024]{2,1,0:T(2,128)(2,1)} %join.1), channel_id=1, replica_groups=mesh['ex'=2,'ey'=16] {'ex','ey'}, dimensions={0} | all-to-all | bytes 262144 | tf_op jit(solution)/shard_map/all_to_all | solution.py:453
  39.8 0.7 %route_back.1 = (bf16[1,32,1024]{2,1,0:T(8,128)(2,1)S(1)}, bf16[1,32,256]{2,1,0:T(8,128)(2,1)S(1)}, bf16[16,1024]{1,0:T(8,128)(2,1)S(1)}, bf16[16,1024]{1,0:T(8,128)(2,1)S(1)}) custom-call(s32[1]{0:T(128)} %bitcast.1.refs_0_.side_ref, bf16[32,1,2,1024]{3,2,1,0:T(2,128)(2,1)S(1)} %bitcast.13, f32[1,32,256]{2,1,0:T(8,128)S(1)} %get-tuple-element.19.disp_ref, ...), custom_call_target="tpu_custom_call" | custom-call | tf_op jit(solution)/shard_map/route_back/pallas_call | solution.py:164
  40.6 1.2 %collective-permute-done.2 = bf16[16,1024]{1,0:T(8,128)(2,1)S(1)} collective-permute-done((bf16[16,1024]{1,0:T(8,128)(2,1)S(1)}, bf16[16,1024]{1,0:T(8,128)(2,1)S(1)}, u32[]{:S(2)}, u32[]{:S(2)}) %collective-permute-start.2) | collective-permute-done | bytes 32800 | tf_op jit(solution)/shard_map/ppermute | solution.py:352
  41.8 1.1 %collective-permute-start.3 = (bf16[16,1024]{1,0:T(8,128)(2,1)S(1)}, bf16[16,1024]{1,0:T(8,128)(2,1)S(1)}, u32[]{:S(2)}, u32[]{:S(2)}) collective-permute-start(bf16[16,1024]{1,0:T(8,128)(2,1)S(1)} %add_convert_fusion.2), channel_id=1, source_target_pairs={{0,1},{1,0},{2,3},{3,2},{4,5},{5,4},{6,7},{7,6},{8,9},{9,8},{10,11... | collective-permute-start | bytes 98312 | tf_op jit(solution)/shard_map/ppermute | solution.py:352
  42.9 0.7 %collective-permute-start.4 = (bf16[16,1024]{1,0:T(8,128)(2,1)S(1)}, bf16[16,1024]{1,0:T(8,128)(2,1)S(1)}, u32[]{:S(2)}, u32[]{:S(2)}) collective-permute-start(bf16[16,1024]{1,0:T(8,128)(2,1)S(1)} %add_convert_fusion.2), channel_id=1, source_target_pairs={{0,2},{1,3},{2,0},{3,1},{4,6},{5,7},{6,4},{7,5},{8,10},{9,11},{10,... | collective-permute-start | bytes 98312 | tf_op jit(solution)/shard_map/ppermute | solution.py:352
  43.6 1.8 %collective-permute-start.5 = (bf16[16,1024]{1,0:T(8,128)(2,1)S(1)}, bf16[16,1024]{1,0:T(8,128)(2,1)S(1)}, u32[]{:S(2)}, u32[]{:S(2)}) collective-permute-start(bf16[16,1024]{1,0:T(8,128)(2,1)S(1)} %add_convert_fusion.2), channel_id=1, source_target_pairs={{0,3},{1,2},{2,1},{3,0},{4,7},{5,6},{6,5},{7,4},{8,11},{9,10},{10,... | collective-permute-start | bytes 98312 | tf_op jit(solution)/shard_map/ppermute | solution.py:352
  45.3 0.4 collective-permute-done.3
  45.7 1.4 %collective-permute-done.4 = bf16[16,1024]{1,0:T(8,128)(2,1)S(1)} collective-permute-done((bf16[16,1024]{1,0:T(8,128)(2,1)S(1)}, bf16[16,1024]{1,0:T(8,128)(2,1)S(1)}, u32[]{:S(2)}, u32[]{:S(2)}) %collective-permute-start.4) | collective-permute-done | bytes 32800 | tf_op jit(solution)/shard_map/ppermute | solution.py:352
  47.1 1.2 %collective-permute-done.5 = bf16[16,1024]{1,0:T(8,128)(2,1)S(1)} collective-permute-done((bf16[16,1024]{1,0:T(8,128)(2,1)S(1)}, bf16[16,1024]{1,0:T(8,128)(2,1)S(1)}, u32[]{:S(2)}, u32[]{:S(2)}) %collective-permute-start.5) | collective-permute-done | bytes 32800 | tf_op jit(solution)/shard_map/ppermute | solution.py:352
  48.4 0.5 collective-permute-start.6
  48.9 1.1 %collective-permute-start.7 = (bf16[16,1024]{1,0:T(8,128)(2,1)S(1)}, bf16[16,1024]{1,0:T(8,128)(2,1)S(1)}, u32[]{:S(2)}, u32[]{:S(2)}) collective-permute-start(bf16[16,1024]{1,0:T(8,128)(2,1)S(1)} %add_convert_fusion.1), channel_id=1, source_target_pairs={{0,8},{1,9},{2,10},{3,11},{4,12},{5,13},{6,14},{7,15},{8,0},{9,1},... | collective-permute-start | bytes 98312 | tf_op jit(solution)/shard_map/ppermute | solution.py:352
  50.1 2.8 %collective-permute-start.8 = (bf16[16,1024]{1,0:T(8,128)(2,1)S(1)}, bf16[16,1024]{1,0:T(8,128)(2,1)S(1)}, u32[]{:S(2)}, u32[]{:S(2)}) collective-permute-start(bf16[16,1024]{1,0:T(8,128)(2,1)S(1)} %add_convert_fusion.1), channel_id=1, source_target_pairs={{0,12},{1,13},{2,14},{3,15},{4,8},{5,9},{6,10},{7,11},{8,4},{9,5},... | collective-permute-start | bytes 98312 | tf_op jit(solution)/shard_map/ppermute | solution.py:352
  52.9 0.9 %collective-permute-done.7 = bf16[16,1024]{1,0:T(8,128)(2,1)S(1)} collective-permute-done((bf16[16,1024]{1,0:T(8,128)(2,1)S(1)}, bf16[16,1024]{1,0:T(8,128)(2,1)S(1)}, u32[]{:S(2)}, u32[]{:S(2)}) %collective-permute-start.7) | collective-permute-done | bytes 32800 | tf_op jit(solution)/shard_map/ppermute | solution.py:352
  53.7 2.0 %collective-permute-done.8 = bf16[16,1024]{1,0:T(8,128)(2,1)S(1)} collective-permute-done((bf16[16,1024]{1,0:T(8,128)(2,1)S(1)}, bf16[16,1024]{1,0:T(8,128)(2,1)S(1)}, u32[]{:S(2)}, u32[]{:S(2)}) %collective-permute-start.8) | collective-permute-done | bytes 32800 | tf_op jit(solution)/shard_map/ppermute | solution.py:352
  55.9 7.8 %weight_grads.1 = (bf16[2,1024,2048]{2,1,0:T(8,128)(2,1)}, bf16[2,2048,1024]{2,1,0:T(8,128)(2,1)}) custom-call(s32[1]{0:T(128)} %bitcast.1.refs_0_.side_ref, bf16[4,32,1024]{2,1,0:T(8,128)(2,1)S(1)} %bitcast.12, bf16[2,32,2048]{2,1,0:T(8,128)(2,1)S(1)} %get-tuple-element.30.refs_2_, bf16[2,32,2048]{2,1,0:T(8,128)(2,1)S(1)} %get-tuple-element.31.refs_3_), custom_call_target="tpu_custom_call" | custom-call | tf_op jit(solution)/shard_map/weight_grads/pallas_call | solution.py:328
  63.7 1.1 %token_grads.1 = bf16[1,256,1024]{2,1,0:T(8,128)(2,1)} custom-call(f32[1,32,256]{2,1,0:T(8,128)S(1)} %get-tuple-element.19.disp_ref, bf16[1,32,1024]{2,1,0:T(8,128)(2,1)S(1)} %get-tuple-element.26.slot_ref, bf16[1,32,256]{2,1,0:T(8,128)(2,1)S(1)} %get-tuple-element.27.dl_ref, bf16[32,1024]{1,0:T(8,128)(2,1)S(1)} %bitcast.15), custom_call_target="tpu_custom_call" | custom-call | tf_op jit(solution)/shard_map/token_grads/pallas_call | solution.py:193
  64.9 0.7 %maximum_bitcast_fusion.1 = f32[1024,32]{0,1:T(8,128)} fusion(f32[16,1024]{1,0:T(8,128)S(1)} %get-tuple-element.35, f32[16,1024]{1,0:T(8,128)S(1)} %get-tuple-element.34), kind=kLoop, calls=%fused_computation.1 | loop fusion | flops 32768 | bytes 262144 | tf_op jit(solution)/shard_map/transpose | solution.py:463
  (18 shorter events, 0.7 us)
Async XLA Ops:
  17.9 1.6 %collective-permute-start = (bf16[32,2,1024]{2,1,0:T(2,128)(2,1)S(1)}, bf16[32,2,1024]{2,1,0:T(2,128)(2,1)S(1)}, u32[]{:S(2)}, u32[]{:S(2)}) collective-permute-start(bf16[32,2,1024]{2,1,0:T(2,128)(2,1)S(1)} %all_to_all.10), channel_id=1, source_target_pairs={{0,16},{16,0},{1,17},{17,1},{2,18},{18,2},{3,19},{19,3},{4,20},{20... | collective-permute-start | bytes 393224 | tf_op jit(solution)/shard_map/ppermute | solution.py:352
  19.9 19.8 %copy-start = (bf16[1,256,1024]{2,1,0:T(8,128)(2,1)S(1)}, bf16[1,256,1024]{2,1,0:T(8,128)(2,1)}, u32[]{:S(2)}) copy-start(bf16[1,256,1024]{2,1,0:T(8,128)(2,1)} %tok_ref.1) | copy-start | bytes 1572868
  19.9 19.8 %copy-start.1 = (bf16[1,256,1024]{2,1,0:T(8,128)(2,1)S(1)}, bf16[1,256,1024]{2,1,0:T(8,128)(2,1)}, u32[]{:S(2)}) copy-start(bf16[1,256,1024]{2,1,0:T(8,128)(2,1)} %out_ref.1) | copy-start | bytes 1572868
  20.0 43.8 %copy-start.2 = (bf16[1024,32]{0,1:T(8,128)(2,1)S(1)}, bf16[1024,32]{0,1:T(8,128)(2,1)}, u32[]{:S(2)}) copy-start(bf16[1024,32]{0,1:T(8,128)(2,1)} %param.6) | copy-start | bytes 196612
  26.8 1.6 %collective-permute-start.1 = (bf16[2,32,1024]{2,1,0:T(8,128)(2,1)S(1)}, bf16[2,32,1024]{2,1,0:T(8,128)(2,1)S(1)}, u32[]{:S(2)}, u32[]{:S(2)}) collective-permute-start(bf16[2,32,1024]{2,1,0:T(8,128)(2,1)S(1)} %get-tuple-element.24), channel_id=1, source_target_pairs={{0,16},{16,0},{1,17},{17,1},{2,18},{18,2},{3,19},{19,3},{4,20},{20... | collective-permute-start | bytes 393224 | tf_op jit(solution)/shard_map/ppermute | solution.py:352
  40.5 1.3 %collective-permute-start.2 = (bf16[16,1024]{1,0:T(8,128)(2,1)S(1)}, bf16[16,1024]{1,0:T(8,128)(2,1)S(1)}, u32[]{:S(2)}, u32[]{:S(2)}) collective-permute-start(bf16[16,1024]{1,0:T(8,128)(2,1)S(1)} %get-tuple-element.29), channel_id=1, source_target_pairs={{0,16},{16,0},{1,17},{17,1},{2,18},{18,2},{3,19},{19,3},{4,20},{20... | collective-permute-start | bytes 98312 | tf_op jit(solution)/shard_map/ppermute | solution.py:352
  41.8 4.0 %collective-permute-start.3 = (bf16[16,1024]{1,0:T(8,128)(2,1)S(1)}, bf16[16,1024]{1,0:T(8,128)(2,1)S(1)}, u32[]{:S(2)}, u32[]{:S(2)}) collective-permute-start(bf16[16,1024]{1,0:T(8,128)(2,1)S(1)} %add_convert_fusion.2), channel_id=1, source_target_pairs={{0,1},{1,0},{2,3},{3,2},{4,5},{5,4},{6,7},{7,6},{8,9},{9,8},{10,11... | collective-permute-start | bytes 98312 | tf_op jit(solution)/shard_map/ppermute | solution.py:352
  42.9 4.3 %collective-permute-start.4 = (bf16[16,1024]{1,0:T(8,128)(2,1)S(1)}, bf16[16,1024]{1,0:T(8,128)(2,1)S(1)}, u32[]{:S(2)}, u32[]{:S(2)}) collective-permute-start(bf16[16,1024]{1,0:T(8,128)(2,1)S(1)} %add_convert_fusion.2), channel_id=1, source_target_pairs={{0,2},{1,3},{2,0},{3,1},{4,6},{5,7},{6,4},{7,5},{8,10},{9,11},{10,... | collective-permute-start | bytes 98312 | tf_op jit(solution)/shard_map/ppermute | solution.py:352
  43.6 4.8 %collective-permute-start.5 = (bf16[16,1024]{1,0:T(8,128)(2,1)S(1)}, bf16[16,1024]{1,0:T(8,128)(2,1)S(1)}, u32[]{:S(2)}, u32[]{:S(2)}) collective-permute-start(bf16[16,1024]{1,0:T(8,128)(2,1)S(1)} %add_convert_fusion.2), channel_id=1, source_target_pairs={{0,3},{1,2},{2,1},{3,0},{4,7},{5,6},{6,5},{7,4},{8,11},{9,10},{10,... | collective-permute-start | bytes 98312 | tf_op jit(solution)/shard_map/ppermute | solution.py:352
  48.4 4.5 %collective-permute-start.6 = (bf16[16,1024]{1,0:T(8,128)(2,1)S(1)}, bf16[16,1024]{1,0:T(8,128)(2,1)S(1)}, u32[]{:S(2)}, u32[]{:S(2)}) collective-permute-start(bf16[16,1024]{1,0:T(8,128)(2,1)S(1)} %add_convert_fusion.1), channel_id=1, source_target_pairs={{0,4},{1,5},{2,6},{3,7},{4,0},{5,1},{6,2},{7,3},{8,12},{9,13},{10,... | collective-permute-start | bytes 98312 | tf_op jit(solution)/shard_map/ppermute | solution.py:352
  48.9 4.8 %collective-permute-start.7 = (bf16[16,1024]{1,0:T(8,128)(2,1)S(1)}, bf16[16,1024]{1,0:T(8,128)(2,1)S(1)}, u32[]{:S(2)}, u32[]{:S(2)}) collective-permute-start(bf16[16,1024]{1,0:T(8,128)(2,1)S(1)} %add_convert_fusion.1), channel_id=1, source_target_pairs={{0,8},{1,9},{2,10},{3,11},{4,12},{5,13},{6,14},{7,15},{8,0},{9,1},... | collective-permute-start | bytes 98312 | tf_op jit(solution)/shard_map/ppermute | solution.py:352
  50.1 5.7 %collective-permute-start.8 = (bf16[16,1024]{1,0:T(8,128)(2,1)S(1)}, bf16[16,1024]{1,0:T(8,128)(2,1)S(1)}, u32[]{:S(2)}, u32[]{:S(2)}) collective-permute-start(bf16[16,1024]{1,0:T(8,128)(2,1)S(1)} %add_convert_fusion.1), channel_id=1, source_target_pairs={{0,12},{1,13},{2,14},{3,15},{4,8},{5,9},{6,10},{7,11},{8,4},{9,5},... | collective-permute-start | bytes 98312 | tf_op jit(solution)/shard_map/ppermute | solution.py:352
  55.8 9.0 %collective-permute-start.9 = (bf16[16,1024]{1,0:T(8,128)(2,1)S(1)}, bf16[16,1024]{1,0:T(8,128)(2,1)S(1)}, u32[]{:S(2)}, u32[]{:S(2)}) collective-permute-start(bf16[16,1024]{1,0:T(8,128)(2,1)S(1)} %add_convert_fusion), channel_id=1, source_target_pairs={{0,16},{16,0},{1,17},{17,1},{2,18},{18,2},{3,19},{19,3},{4,20},{20... | collective-permute-start | bytes 98312 | tf_op jit(solution)/shard_map/ppermute | solution.py:352
